TPU v7x, 512 devices: a whole 4x8x8 slice. The times are simulated.
512 devices in a mesh: seq: 128 (over z_hi, x, y), slab: 4 (over z_lo, core).
Axes of the slice: x: 4, y: 8, z: 8 (z_hi: 4, z_lo: 2; z = z_hi * 2 + z_lo), core: 2. Of those that a mesh axis runs over, the one named last changes fastest.
Arguments:
- hidden: bfloat16 [12288, 5120], P('seq', 'slab'), may hold values from -130 to 130, as said below
- tangent: bfloat16 [12288, 5120], P('seq', 'slab'), may hold values from -6 to 6
- mod_shift: float32 [5120], P('slab'), may hold values from -2 to 2
- mod_scale: float32 [5120], P('slab'), may hold values from -1.5 to 1.5
- head_weight: bfloat16 [64, 5120], P(None, 'slab'), may hold values from -0.078125 to 0.078125
- head_bias: float32 [64], replicated, may hold values from -2 to 2
- in_weight: bfloat16 [3, 3, 3, 16, 384], replicated, may hold values from -0.3125 to 0.3125
- in_bias: float32 [384], replicated, may hold values from -2 to 2
- norm_gain: float32 [384], replicated, may hold values from 0.1 to 1.9
- mid_weight: bfloat16 [3, 3, 3, 384, 384], P(None, None, None, 'slab'), may hold values from -0.0625 to 0.0625
Outputs:
- features_tangent: bfloat16 [128, 2, 48, 4, 384], P('seq', None, 'slab')
Inputs may be any that keep to these rules, and one draw needn't show every extreme that they name: hidden states of the transformer's last block.
All inputs are finite; a program needn't handle non-finite values.
Results may differ from a plain program's by a relative error of at most 0.008.
Values may be sent and summed in bfloat16 or wider, within the bound.
A program may use at most 64 MiB of HBM per device.

v0:
```python
import jax
import jax.numpy as jnp
from jax import lax
from jax.sharding import PartitionSpec as P

D = 5120
ZC = 16
CG = 8
FR_DEV = 2
HT = 24
CT = 2


def from_partner(block, axis, distance):
    count = lax.axis_size(axis)
    route = []
    for low in range(count):
        high = low | 1 << distance
        if high != low and high < count:
            route += [(low, high), (high, low)]
    return lax.ppermute(block, axis, route)


def from_behind(array, axis, by):
    count = lax.axis_size(axis)
    return lax.ppermute(array, axis, [(i, (i + by) % count) for i in range(count)])


def with_halo(array, sides, width):
    for axis, dim in sides:
        count, length = (lax.axis_size(axis), array.shape[dim])
        up = [(i, (i + 1) % count) for i in range(count)]
        down = [(j, i) for i, j in up]
        last = lax.slice_in_dim(array, length - width, length, axis=dim)
        first = lax.slice_in_dim(array, 0, width, axis=dim)
        before = lax.ppermute(last, axis, up)
        after = lax.ppermute(first, axis, down)
        array = jnp.concatenate([before, array, after], axis=dim)
    return array


def tap_offsets():
    return [
        (frame_tap, row_tap, col_tap)
        for frame_tap in range(3)
        for row_tap in range(3)
        for col_tap in range(3)
    ]


def conv_lowered(padded, weight, frames, height, span_cols):
    pieces = []
    for frame_tap, row_tap, col_tap in tap_offsets():
        pieces.append(
            padded[
                ...,
                frame_tap : frame_tap + frames,
                row_tap : row_tap + height,
                col_tap : col_tap + span_cols,
                :,
            ]
        )
    stacked = jnp.concatenate(pieces, axis=-1)
    flat_weight = weight.reshape(-1, weight.shape[-1])
    return jnp.dot(stacked, flat_weight, preferred_element_type=jnp.float32)


def conv_by_taps(padded, weight, frames, height, span_cols):
    running = jnp.zeros((frames, height, span_cols, weight.shape[-1]), jnp.float32)
    for frame_tap, row_tap, col_tap in tap_offsets():
        window = padded[
            frame_tap : frame_tap + frames,
            row_tap : row_tap + height,
            col_tap : col_tap + span_cols,
            :,
        ]
        running = running + jnp.dot(
            window, weight[frame_tap, row_tap, col_tap], preferred_element_type=jnp.float32
        )
    return running


def norm_tangent(features, dfeatures, norm_gain):
    scale_inv = lax.rsqrt(jnp.mean(features * features, axis=-1, keepdims=True) + 1e-06)
    along = jnp.mean(features * dfeatures, axis=-1, keepdims=True)
    normed_feat = norm_gain * features * scale_inv
    tangent_feat = norm_gain * scale_inv * (dfeatures - features * scale_inv * scale_inv * along)
    sigmoid_u = jax.nn.sigmoid(normed_feat)
    return (sigmoid_u * (1.0 + normed_feat * (1.0 - sigmoid_u)) * tangent_feat).astype(jnp.bfloat16)


def relayout(blocks, position, trade):
    for bit in range(CG.bit_length() - 1):
        stride = 1 << bit
        shaped = blocks.reshape((CG // (2 * stride), 2, stride) + blocks.shape[1:])
        lower = shaped[:, 0]
        upper = shaped[:, 1]
        keep_lower = jnp.bitwise_and(jnp.right_shift(position, bit), 1) == 0
        outgoing = jnp.where(keep_lower, upper, lower)
        incoming = trade(outgoing, bit)
        new_lower = jnp.where(keep_lower, lower, incoming)
        new_upper = jnp.where(keep_lower, incoming, upper)
        blocks = jnp.stack([new_lower, new_upper], axis=1).reshape(blocks.shape)
    return blocks


def keep_columns(values, position, width, dim):
    span = values.shape[dim]
    inner = span - 2 * width
    column = position * inner - width + jnp.arange(span, dtype=jnp.int32)
    inside = (column >= 0) & (column < CG * inner)
    shape = [1] * values.ndim
    shape[dim] = span
    return jnp.where(inside.reshape(shape), values, jnp.zeros_like(values))


def earlier_frames(values, frame_dim, shifter, frame_group):
    moved = shifter(values, 1)
    pieces = [jnp.where(frame_group >= 1, moved, jnp.zeros_like(moved))]
    return jnp.concatenate(pieces + [values], axis=frame_dim)


def shards(
    hidden,
    tangent,
    mod_shift,
    mod_scale,
    head_weight,
    head_bias,
    in_weight,
    in_bias,
    norm_gain,
    mid_weight,
):
    states = hidden.astype(jnp.float32)
    tangents = tangent.astype(jnp.float32)
    moment_sums = lax.psum(
        (
            jnp.sum(states, axis=1),
            jnp.sum(states * states, axis=1),
            jnp.sum(tangents, axis=1),
            jnp.sum(states * tangents, axis=1),
        ),
        "slab",
    )
    token_mean = moment_sums[0][:, None] / D
    variance = moment_sums[1][:, None] / D - token_mean * token_mean
    inverse = lax.rsqrt(variance + 1e-06)
    mean_tangent = moment_sums[2][:, None] / D
    project = inverse * (moment_sums[3][:, None] / D - token_mean * mean_tangent)
    normed = (states - token_mean) * inverse
    dnormed = inverse * (tangents - mean_tangent - normed * project)
    scaling = 1.0 + mod_scale
    modulated = (normed * scaling + mod_shift).astype(jnp.bfloat16)
    dmodulated = (dnormed * scaling).astype(jnp.bfloat16)
    contract = (((1,), (1,)), ((), ()))
    partial_value = jnp.concatenate(
        [
            lax.dot_general(modulated, head_weight, contract, preferred_element_type=jnp.float32),
            lax.dot_general(dmodulated, head_weight, contract, preferred_element_type=jnp.float32),
        ],
        axis=1,
    )
    bias_vector = jnp.concatenate([head_bias, jnp.zeros_like(head_bias)])
    seq_count = lax.axis_size("seq")
    seq_index = lax.axis_index("seq")
    slab_index = lax.axis_index("slab")
    relay_position = seq_index % CG
    rotated = (seq_index - CG // 2 + seq_count) % seq_count
    position = rotated % CG
    frame_group = rotated // CG
    shard_rows = partial_value.shape[0] // (CG * CT)
    summed = lax.psum(partial_value, "slab")
    values = (summed + bias_vector).astype(jnp.bfloat16)
    packed = values.reshape(shard_rows, CG, CT, values.shape[1]).transpose(1, 0, 2, 3)

    def trade_whole(half, bit):
        return from_partner(half, "seq", bit)

    arrived = relayout(packed, relay_position, trade_whole)
    arrived = from_behind(arrived, "seq", CG // 2)
    token_grid = arrived.reshape(FR_DEV, HT, CT, 2, 2, 2, ZC)
    latents = token_grid.transpose(3, 0, 1, 4, 2, 5, 6).reshape(2, FR_DEV, 2 * HT, 2 * CT, ZC)
    margin_width = 1
    depth = 2 * margin_width
    latent_rim = with_halo(latents, (("seq", 3),), margin_width)
    latent_rim = keep_columns(latent_rim, position, margin_width, 3)

    def latent_shift(tail, back):
        return from_behind(tail, "seq", back * CG)

    latent_ext = earlier_frames(latent_rim, 1, latent_shift, frame_group)
    padded = jnp.pad(latent_ext, ((0, 0), (0, 0), (1, 1), (0, 0), (0, 0)))
    out_frames = FR_DEV + depth - 2
    out_width = 2 * CT + 2 * (margin_width - 1)
    conv_pair = conv_lowered(padded, in_weight, out_frames, 2 * HT, out_width)
    features = conv_pair[0] + in_bias
    dfeatures = conv_pair[1]
    act_tangent = norm_tangent(features, dfeatures, norm_gain)
    sides = with_halo(act_tangent, (("seq", 2),), 1)
    sides = keep_columns(sides, position, 1, 2)

    def tangent_shift(tail, back):
        return from_behind(tail, "seq", back * CG)

    widened = earlier_frames(sides, 0, tangent_shift, frame_group)
    residual = dfeatures
    share_in_ch = mid_weight.shape[3]
    widened_share = lax.dynamic_slice_in_dim(widened, slab_index * share_in_ch, share_in_ch, 3)
    tangent_pad = jnp.pad(widened_share, ((0, 0), (1, 1), (0, 0), (0, 0)))
    out_conv = conv_by_taps(tangent_pad, mid_weight, FR_DEV, 2 * HT, 2 * CT)
    row_part = lax.psum_scatter(
        out_conv.astype(jnp.bfloat16), "slab", scatter_dimension=1, tiled=True
    ).astype(jnp.float32)
    share_rows = row_part.shape[1]
    residual = lax.dynamic_slice_in_dim(residual, slab_index * share_rows, share_rows, 1)
    return (row_part + residual).astype(jnp.bfloat16)[None]


def solution(mesh):
    return jax.shard_map(
        shards,
        mesh=mesh,
        in_specs=(
            P("seq", "slab"),
            P("seq", "slab"),
            P("slab"),
            P("slab"),
            P(None, "slab"),
            P(),
            P(),
            P(),
            P(),
            P(None, None, None, "slab", None),
        ),
        out_specs=P("seq", None, "slab", None, None),
        check_vma=False,
    )
```

profile of v0, /device:TPU:1, one launch (start us, length us, event | category | flops | bytes accessed | tf_op | source)
XLA Modules:
  0.0 205.9 jit_solution(13053193458192945805)
XLA Ops:
  6.5 0.8 broadcast_add_fusion
  7.3 1.3 fusion.15
  8.6 11.9 %all-reduce.4 = (f32[96]{0:T(128)S(1)}, f32[96]{0:T(128)S(1)}, f32[96]{0:T(128)S(1)}, f32[96]{0:T(128)S(1)}) all-reduce(f32[96]{0:T(128)S(1)} %get-tuple-element.8, f32[96]{0:T(128)S(1)} %get-tuple-element.9, f32[96]{0:T(128)S(1)} %get-tuple-element.10, f32[96]{0:T(128)S(1)} %get-tuple-element.7), channel_id=1, replica_groups=mesh['seq'=128,'slab'=4] {'slab'}, use_global_device_ids=true, to_apply=%region_7.0 | all-reduce | flops 384 | bytes 3072 | tf_op jit(solution)/shard_map/psum | solution.py:137
  20.5 1.3 fusion.18
  21.9 1.5 fusion.24
  23.5 10.9 %psum.39 = f32[96,128]{1,0:T(8,128)S(1)} all-reduce(f32[96,128]{1,0:T(8,128)S(1)} %pad_maximum_fusion.1), channel_id=1, replica_groups=mesh['seq'=128,'slab'=4] {'slab'}, use_global_device_ids=true, to_apply=%region_8.9 | all-reduce | flops 12288 | bytes 98304 | tf_op jit(solution)/shard_map/psum | solution.py:173
  34.5 1.9 collective-permute-start
  36.4 2.5 %collective-permute-done = bf16[4,1,6,2,128]{4,3,2,0,1:T(2,128)(2,1)S(1)} collective-permute-done((bf16[4,1,6,2,128]{4,3,2,0,1:T(2,128)(2,1)S(1)}, bf16[4,1,6,2,128]{4,3,2,0,1:T(2,128)(2,1)S(1)}, u32[]{:S(2)}, u32[]{:S(2)}) %collective-permute-start) | collective-permute-done | bytes 12320 | tf_op jit(solution)/shard_map/ppermute | solution.py:21
  39.0 1.9 collective-permute-start.1
  40.9 3.4 %collective-permute-done.1 = bf16[2,2,6,2,128]{4,3,2,1,0:T(2,128)(2,1)S(1)} collective-permute-done((bf16[2,2,6,2,128]{4,3,2,1,0:T(2,128)(2,1)S(1)}, bf16[2,2,6,2,128]{4,3,2,1,0:T(2,128)(2,1)S(1)}, u32[]{:S(2)}, u32[]{:S(2)}) %collective-permute-start.1) | collective-permute-done | bytes 12320 | tf_op jit(solution)/shard_map/ppermute | solution.py:21
  44.5 3.6 %collective-permute-start.2 = (bf16[1,4,6,2,128]{4,3,2,1,0:T(2,128)(2,1)S(1)}, bf16[1,4,6,2,128]{4,3,2,1,0:T(2,128)(2,1)S(1)}, u32[]{:S(2)}, u32[]{:S(2)}) collective-permute-start(bf16[1,4,6,2,128]{4,3,2,1,0:T(2,128)(2,1)S(1)} %broadcast_select_fusion.10), channel_id=1, source_target_pairs={{0,16},{16,0},{4,20},{20,4},{8,24},{24,8},{12,28},{28,12},{32,48},... | collective-permute-start | bytes 36872 | tf_op jit(solution)/shard_map/ppermute | solution.py:21
  48.1 4.7 %collective-permute-done.2 = bf16[1,4,6,2,128]{4,3,2,1,0:T(2,128)(2,1)S(1)} collective-permute-done((bf16[1,4,6,2,128]{4,3,2,1,0:T(2,128)(2,1)S(1)}, bf16[1,4,6,2,128]{4,3,2,1,0:T(2,128)(2,1)S(1)}, u32[]{:S(2)}, u32[]{:S(2)}) %collective-permute-start.2) | collective-permute-done | bytes 12320 | tf_op jit(solution)/shard_map/ppermute | solution.py:21
  52.9 3.6 %collective-permute-start.3 = (bf16[8,6,2,128]{3,2,1,0:T(2,128)(2,1)S(1)}, bf16[8,6,2,128]{3,2,1,0:T(2,128)(2,1)S(1)}, u32[]{:S(2)}, u32[]{:S(2)}) collective-permute-start(bf16[8,6,2,128]{3,2,1,0:T(2,128)(2,1)S(1)} %bitcast.301), channel_id=1, source_target_pairs={{0,16},{4,20},{8,24},{12,28},{16,32},{20,36},{24,40},{28,44},{32,4... | collective-permute-start | bytes 73736 | tf_op jit(solution)/shard_map/ppermute | solution.py:26
  56.6 10.9 %collective-permute-done.3 = bf16[8,6,2,128]{3,2,1,0:T(2,128)(2,1)S(1)} collective-permute-done((bf16[8,6,2,128]{3,2,1,0:T(2,128)(2,1)S(1)}, bf16[8,6,2,128]{3,2,1,0:T(2,128)(2,1)S(1)}, u32[]{:S(2)}, u32[]{:S(2)}) %collective-permute-start.3) | collective-permute-done | bytes 24608 | tf_op jit(solution)/shard_map/ppermute | solution.py:26
  67.8 2.3 %collective-permute-start.4 = (bf16[2,2,48,1,16]{4,2,3,1,0:T(8,128)(2,1)S(1)}, bf16[2,2,48,1,16]{4,2,3,1,0:T(8,128)(2,1)S(1)}, u32[]{:S(2)}, u32[]{:S(2)}) collective-permute-start(bf16[2,2,48,1,16]{4,2,3,1,0:T(8,128)(2,1)S(1)} %get-tuple-element.44), channel_id=1, source_target_pairs={{0,4},{4,8},{8,12},{12,16},{16,20},{20,24},{24,28},{28,32},{32,36}... | collective-permute-start | bytes 18440 | tf_op jit(solution)/shard_map/ppermute | solution.py:36
  70.1 9.3 %collective-permute-start.5 = (bf16[2,2,48,1,16]{4,2,3,1,0:T(8,128)(2,1)S(1)}, bf16[2,2,48,1,16]{4,2,3,1,0:T(8,128)(2,1)S(1)}, u32[]{:S(2)}, u32[]{:S(2)}) collective-permute-start(bf16[2,2,48,1,16]{4,2,3,1,0:T(8,128)(2,1)S(1)} %get-tuple-element.45), channel_id=1, source_target_pairs={{4,0},{8,4},{12,8},{16,12},{20,16},{24,20},{28,24},{32,28},{36,32}... | collective-permute-start | bytes 18440 | tf_op jit(solution)/shard_map/ppermute | solution.py:37
  79.5 1.1 collective-permute-done.5
  80.7 1.9 collective-permute-start.6
  82.6 14.3 %collective-permute-done.6 = bf16[2,2,48,6,16]{4,2,3,1,0:T(8,128)(2,1)S(1)} collective-permute-done((bf16[2,2,48,6,16]{4,2,3,1,0:T(8,128)(2,1)S(1)}, bf16[2,2,48,6,16]{4,2,3,1,0:T(8,128)(2,1)S(1)}, u32[]{:S(2)}, u32[]{:S(2)}) %collective-permute-start.6) | collective-permute-done | bytes 36896 | tf_op jit(solution)/shard_map/ppermute | solution.py:26
  97.1 1.3 fusion.28
  98.4 2.0 pad_slice_fusion.6
  100.4 4.4 %concatenate.26 = bf16[2,2,48,4,432]{4,2,3,1,0:T(8,128)(2,1)S(1)} concatenate(bf16[2,2,48,4,16]{4,2,3,1,0:T(8,128)(2,1)} %get-tuple-element.32, bf16[2,2,48,4,16]{4,2,3,1,0:T(8,128)(2,1)S(1)} %get-tuple-element.16, bf16[2,2,48,4,16]{4,2,3,1,0:T(8,128)(2,1)S(1)} %get-tuple-element.17, bf16[2,2,48,4,16]{4,2,3,1,0:T(8,128)(2,1)} %get-tuple-element.41, ...), dimensions={4} | concatenate | bytes 1327104 | tf_op jit(solution)/shard_map/concatenate | solution.py:63
  104.9 0.6 fusion.148
  105.5 0.2 multiply_reduce_fusion
  105.8 0.4 fusion.5
  106.2 2.1 collective-permute-start.7
  108.3 9.7 %collective-permute-start.8 = (bf16[2,48,1,384]{3,1,2,0:T(8,128)(2,1)S(1)}, bf16[2,48,1,384]{3,1,2,0:T(8,128)(2,1)S(1)}, u32[]{:S(2)}, u32[]{:S(2)}) collective-permute-start(bf16[2,48,1,384]{3,1,2,0:T(8,128)(2,1)S(1)} %get-tuple-element.37), channel_id=1, source_target_pairs={{4,0},{8,4},{12,8},{16,12},{20,16},{24,20},{28,24},{32,28},{36,32}... | collective-permute-start | bytes 221192 | tf_op jit(solution)/shard_map/ppermute | solution.py:37
  118.0 1.4 collective-permute-done.8
  119.4 0.9 maximum_select_fusion
  120.3 1.9 collective-permute-start.9
  122.2 14.2 %collective-permute-done.9 = bf16[2,48,6,384]{3,1,2,0:T(8,128)(2,1)} collective-permute-done((bf16[2,48,6,384]{3,1,2,0:T(8,128)(2,1)}, bf16[2,48,6,384]{3,1,2,0:T(8,128)(2,1)}, u32[]{:S(2)}, u32[]{:S(2)}) %collective-permute-start.9) | collective-permute-done | bytes 442400 | tf_op jit(solution)/shard_map/ppermute | solution.py:26
  136.3 1.1 broadcast_select_fusion
  137.4 1.2 fusion.17
  138.6 0.2 fusion.47
  138.8 0.2 convolution_add_fusion.16
  139.0 0.2 convolution_add_fusion.15
  139.2 0.2 convolution_add_fusion.25
  139.5 0.2 convolution_add_fusion.24
  139.7 0.2 convolution_add_fusion.23
  139.9 0.2 convolution_add_fusion.14
  140.1 0.2 convolution_add_fusion.13
  140.4 0.2 convolution_add_fusion.12
  140.6 0.2 convolution_add_fusion.11
  140.8 0.2 convolution_add_fusion.10
  141.0 0.2 convolution_add_fusion.9
  141.3 0.2 convolution_add_fusion.22
  141.5 0.2 convolution_add_fusion.21
  141.7 0.2 convolution_add_fusion.20
  141.9 0.2 convolution_add_fusion.8
  142.2 0.2 convolution_add_fusion.7
  142.4 0.2 convolution_add_fusion.6
  142.6 0.2 convolution_add_fusion.5
  142.8 0.2 convolution_add_fusion.4
  143.1 0.2 convolution_add_fusion.3
  143.3 0.2 convolution_add_fusion.19
  143.5 0.2 convolution_add_fusion.18
  143.8 0.2 convolution_add_fusion.17
  144.0 0.2 convolution_add_fusion.2
  144.2 0.2 convolution_add_fusion.1
  144.4 0.2 fusion
  144.7 0.8 copy.83
  145.5 1.3 dynamic-slice.1
  147.5 50.0 %all-reduce.7.cloned.1.call-done = bf16[2,48,4,384]{3,2,0,1:T(4,128)(2,1)} async-done(((bf16[2,48,4,384]{3,2,0,1:T(4,128)(2,1)}), bf16[2,48,4,384]{3,2,0,1:T(4,128)(2,1)}) %all-reduce.7.cloned.1.call-update) | async-done | bytes 294928
  197.5 1.6 fusion.49
  (40 shorter events, 1.2 us)
Async XLA Ops:
  6.5 98.3 %copy-start = (bf16[3,3,3,16,384]{4,3,2,1,0:T(8,128)(2,1)S(1)}, bf16[3,3,3,16,384]{4,3,2,1,0:T(8,128)(2,1)}, u32[]{:S(2)}) copy-start(bf16[3,3,3,16,384]{4,3,2,1,0:T(8,128)(2,1)} %param.16) | copy-start | bytes 995332
  6.5 27.8 %copy-start.4 = (f32[64]{0:T(128)S(1)}, f32[64]{0:T(128)}, u32[]{:S(2)}) copy-start(f32[64]{0:T(128)} %param.15) | copy-start | bytes 772
  6.5 191.0 %all-reduce.7.cloned.1.call-start = ((), (), s32[]{:S(2)}) async-start(), calls=%async_computation | async-start | bytes 589824
  34.5 4.4 %collective-permute-start = (bf16[4,1,6,2,128]{4,3,2,0,1:T(2,128)(2,1)S(1)}, bf16[4,1,6,2,128]{4,3,2,0,1:T(2,128)(2,1)S(1)}, u32[]{:S(2)}, u32[]{:S(2)}) collective-permute-start(bf16[4,1,6,2,128]{4,3,2,0,1:T(2,128)(2,1)S(1)} %broadcast_select_fusion.4), channel_id=1, source_target_pairs={{0,4},{4,0},{8,12},{12,8},{16,20},{20,16},{24,28},{28,24},{32,36},... | collective-permute-start | bytes 36872 | tf_op jit(solution)/shard_map/ppermute | solution.py:21
  39.0 5.3 %collective-permute-start.1 = (bf16[2,2,6,2,128]{4,3,2,1,0:T(2,128)(2,1)S(1)}, bf16[2,2,6,2,128]{4,3,2,1,0:T(2,128)(2,1)S(1)}, u32[]{:S(2)}, u32[]{:S(2)}) collective-permute-start(bf16[2,2,6,2,128]{4,3,2,1,0:T(2,128)(2,1)S(1)} %broadcast_select_fusion.7), channel_id=1, source_target_pairs={{0,8},{8,0},{4,12},{12,4},{16,24},{24,16},{20,28},{28,20},{32,40},... | collective-permute-start | bytes 36872 | tf_op jit(solution)/shard_map/ppermute | solution.py:21
  44.5 8.3 %collective-permute-start.2 = (bf16[1,4,6,2,128]{4,3,2,1,0:T(2,128)(2,1)S(1)}, bf16[1,4,6,2,128]{4,3,2,1,0:T(2,128)(2,1)S(1)}, u32[]{:S(2)}, u32[]{:S(2)}) collective-permute-start(bf16[1,4,6,2,128]{4,3,2,1,0:T(2,128)(2,1)S(1)} %broadcast_select_fusion.10), channel_id=1, source_target_pairs={{0,16},{16,0},{4,20},{20,4},{8,24},{24,8},{12,28},{28,12},{32,48},... | collective-permute-start | bytes 36872 | tf_op jit(solution)/shard_map/ppermute | solution.py:21
  52.9 14.6 %collective-permute-start.3 = (bf16[8,6,2,128]{3,2,1,0:T(2,128)(2,1)S(1)}, bf16[8,6,2,128]{3,2,1,0:T(2,128)(2,1)S(1)}, u32[]{:S(2)}, u32[]{:S(2)}) collective-permute-start(bf16[8,6,2,128]{3,2,1,0:T(2,128)(2,1)S(1)} %bitcast.301), channel_id=1, source_target_pairs={{0,16},{4,20},{8,24},{12,28},{16,32},{20,36},{24,40},{28,44},{32,4... | collective-permute-start | bytes 73736 | tf_op jit(solution)/shard_map/ppermute | solution.py:26
  67.8 11.7 %collective-permute-start.4 = (bf16[2,2,48,1,16]{4,2,3,1,0:T(8,128)(2,1)S(1)}, bf16[2,2,48,1,16]{4,2,3,1,0:T(8,128)(2,1)S(1)}, u32[]{:S(2)}, u32[]{:S(2)}) collective-permute-start(bf16[2,2,48,1,16]{4,2,3,1,0:T(8,128)(2,1)S(1)} %get-tuple-element.44), channel_id=1, source_target_pairs={{0,4},{4,8},{8,12},{12,16},{16,20},{20,24},{24,28},{28,32},{32,36}... | collective-permute-start | bytes 18440 | tf_op jit(solution)/shard_map/ppermute | solution.py:36
  70.1 10.5 %collective-permute-start.5 = (bf16[2,2,48,1,16]{4,2,3,1,0:T(8,128)(2,1)S(1)}, bf16[2,2,48,1,16]{4,2,3,1,0:T(8,128)(2,1)S(1)}, u32[]{:S(2)}, u32[]{:S(2)}) collective-permute-start(bf16[2,2,48,1,16]{4,2,3,1,0:T(8,128)(2,1)S(1)} %get-tuple-element.45), channel_id=1, source_target_pairs={{4,0},{8,4},{12,8},{16,12},{20,16},{24,20},{28,24},{32,28},{36,32}... | collective-permute-start | bytes 18440 | tf_op jit(solution)/shard_map/ppermute | solution.py:37
  80.7 16.3 %collective-permute-start.6 = (bf16[2,2,48,6,16]{4,2,3,1,0:T(8,128)(2,1)S(1)}, bf16[2,2,48,6,16]{4,2,3,1,0:T(8,128)(2,1)S(1)}, u32[]{:S(2)}, u32[]{:S(2)}) collective-permute-start(bf16[2,2,48,6,16]{4,2,3,1,0:T(8,128)(2,1)S(1)} %maximum_select_fusion.1), channel_id=1, source_target_pairs={{0,32},{4,36},{8,40},{12,44},{16,48},{20,52},{24,56},{28,60},{32,6... | collective-permute-start | bytes 110600 | tf_op jit(solution)/shard_map/ppermute | solution.py:26
  104.8 0.7 copy-start.2
  104.9 0.9 copy-start.3
  106.2 32.4 %copy-start.1 = (bf16[3,3,3,96,384]{4,3,2,1,0:T(8,128)(2,1)S(1)}, bf16[3,3,3,96,384]{4,3,2,1,0:T(8,128)(2,1)}, u32[]{:S(2)}) copy-start(bf16[3,3,3,96,384]{4,3,2,1,0:T(8,128)(2,1)} %param.19) | copy-start | bytes 5971972
  106.2 11.8 %collective-permute-start.7 = (bf16[2,48,1,384]{3,1,2,0:T(8,128)(2,1)S(1)}, bf16[2,48,1,384]{3,1,2,0:T(8,128)(2,1)S(1)}, u32[]{:S(2)}, u32[]{:S(2)}) collective-permute-start(bf16[2,48,1,384]{3,1,2,0:T(8,128)(2,1)S(1)} %get-tuple-element.36), channel_id=1, source_target_pairs={{0,4},{4,8},{8,12},{12,16},{16,20},{20,24},{24,28},{28,32},{32,36}... | collective-permute-start | bytes 221192 | tf_op jit(solution)/shard_map/ppermute | solution.py:36
  108.3 11.1 %collective-permute-start.8 = (bf16[2,48,1,384]{3,1,2,0:T(8,128)(2,1)S(1)}, bf16[2,48,1,384]{3,1,2,0:T(8,128)(2,1)S(1)}, u32[]{:S(2)}, u32[]{:S(2)}) collective-permute-start(bf16[2,48,1,384]{3,1,2,0:T(8,128)(2,1)S(1)} %get-tuple-element.37), channel_id=1, source_target_pairs={{4,0},{8,4},{12,8},{16,12},{20,16},{24,20},{28,24},{32,28},{36,32}... | collective-permute-start | bytes 221192 | tf_op jit(solution)/shard_map/ppermute | solution.py:37
  120.3 16.1 %collective-permute-start.9 = (bf16[2,48,6,384]{3,1,2,0:T(8,128)(2,1)}, bf16[2,48,6,384]{3,1,2,0:T(8,128)(2,1)}, u32[]{:S(2)}, u32[]{:S(2)}) collective-permute-start(bf16[2,48,6,384]{3,1,2,0:T(8,128)(2,1)} %maximum_select_fusion), channel_id=1, source_target_pairs={{0,32},{4,36},{8,40},{12,44},{16,48},{20,52},{24,56},{28,60},{32,6... | collective-permute-start | bytes 1327112 | tf_op jit(solution)/shard_map/ppermute | solution.py:26
Sparse Core Ops, SparseCore 0:
  145.6 51.8 all-reduce.6
where the time goes:
time: 207 us; the launch traced here: 206 us
  waiting for transfers between devices  103 us (50%)
  starting transfers between devices  38.3 us (19%)
  blocking collectives  22.8 us (11%)
  between operations  14.7 us (7%)
  other arithmetic  9.31 us (4%)
  matrix products  9.28 us (4%)
  local copies, waits for them, and re-layouts  9.02 us (4%)
    unnamed x2, waiting for transfers between devices  50 us
    ppermute x3, waiting for transfers between devices, from_behind(): lax.ppermute(array, axis, [(i, (i + by) % count) for i in range(count)])  39.4 us
    ppermute x2, starting transfers between devices, with_halo(): after = lax.ppermute(first, axis, down)  19 us
    psum x1, blocking collectives, shards(): lax.psum((jnp.sum(states, axis=1), jnp.sum(states * states, axis=1), jnp....  11.9 us
    psum x1, blocking collectives, shards(): summed = lax.psum(partial_value, 'slab')  10.9 us
    ppermute x3, waiting for transfers between devices, from_partner(): return lax.ppermute(block, axis, route)  10.6 us
    ppermute x3, starting transfers between devices, from_partner(): return lax.ppermute(block, axis, route)  7.48 us
    ppermute x3, starting transfers between devices, from_behind(): lax.ppermute(array, axis, [(i, (i + by) % count) for i in range(count)])  7.47 us
  transfers between devices with their start and end apart: 11, of which 9 were waited for; matrix products, arithmetic and copies ran while one was open for 1% of the time, Pallas kernels for 0%

commit v1 on v0

v1 whole, which is shorter than its diff:
```python
import jax
import jax.numpy as jnp
from jax import lax
from jax.experimental import pallas as pl
from jax.experimental.pallas import tpu as pltpu
from jax.sharding import PartitionSpec as P

D = 5120
CH = 384
CG = 8
GROUPS = 16
SLABS = 4
TOK = 96
DS = D // SLABS
SHARE = CH // SLABS
F32 = jnp.float32
BF16 = jnp.bfloat16
MESH = pl.DeviceIdType.MESH
NT = (((1,), (1,)), ((), ()))


def lanes_of(shape):
    return lax.broadcasted_iota(jnp.int32, shape, len(shape) - 1)


def head_partials(xv, dxv, hwv, scale_ref, shift_ref, send):
    x = xv[...]
    dx = dxv[...]
    xf = x.astype(F32)
    dxf = dx.astype(F32)
    sums = [
        jnp.sum(xf, axis=1, keepdims=True),
        jnp.sum(xf * xf, axis=1, keepdims=True),
        jnp.sum(dxf, axis=1, keepdims=True),
        jnp.sum(xf * dxf, axis=1, keepdims=True),
    ]
    lane = lanes_of((TOK, 128))
    moments = jnp.zeros((TOK, 128), F32)
    for k, value in enumerate(sums):
        moments = jnp.where(lane == k, value, moments)
    moments = jnp.concatenate([moments, jnp.zeros((128 - TOK, 128), F32)], axis=0)
    w = hwv[...]
    wf = w.astype(F32) * (1.0 + scale_ref[...].reshape(1, DS))
    hi = wf.astype(BF16)
    lo = (wf - hi.astype(F32)).astype(BF16)
    shift = shift_ref[...].reshape(1, DS)
    shift_hi = shift.astype(BF16).astype(F32)
    shift_mid = (shift - shift_hi).astype(BF16).astype(F32)
    shift_lo = shift - shift_hi - shift_mid
    row = lax.broadcasted_iota(jnp.int32, (16, DS), 0)
    extra = jnp.where(row == 0, 1.0, 0.0)
    extra = jnp.where(row == 1, shift_hi, extra)
    extra = jnp.where(row == 2, shift_mid, extra)
    extra = jnp.where(row == 3, shift_lo, extra).astype(BF16)
    both = jnp.concatenate([x, dx, extra], axis=0)
    split = jnp.concatenate([hi, lo], axis=0)
    prod = lax.dot_general(both, split, NT, preferred_element_type=F32)
    prod = prod + pltpu.roll(prod, 64, 1)
    twice = jnp.concatenate([w, w], axis=0)
    shifted = lax.dot_general(extra, twice, NT, preferred_element_type=F32)
    lane1 = lanes_of((8, 128))
    ones_row = jnp.broadcast_to(prod[2 * TOK : 2 * TOK + 1], (8, 128))
    shift_row = jnp.broadcast_to(shifted[1:2] + shifted[2:3] + shifted[3:4], (8, 128))
    send[0:TOK, :] = jnp.where(lane < 64, prod[0:TOK], prod[TOK : 2 * TOK])
    send[TOK : TOK + 8, :] = jnp.transpose(moments)[0:8]
    send[TOK + 8 : TOK + 16, :] = jnp.where(lane1 < 64, ones_row, shift_row)


def head_finish(total, bias):
    part = total[0:TOK]
    moments = jnp.concatenate([total[TOK : TOK + 8], jnp.zeros((120, 128), F32)], axis=0)
    moments = jnp.transpose(moments)[0:TOK]
    const = total[TOK + 8 : TOK + 9]
    mean = moments[:, 0:1] / D
    variance = moments[:, 1:2] / D - mean * mean
    inverse = lax.rsqrt(variance + 1e-06)
    mean_tangent = moments[:, 2:3] / D
    project = inverse * (moments[:, 3:4] / D - mean * mean_tangent)
    lane = lanes_of((TOK, 128))
    lane1 = lanes_of((1, 128))
    turned = pltpu.roll(jnp.broadcast_to(const, (8, 128)), 64, 1)[0:1]
    weight_sum = jnp.where(lane1 < 64, const, turned)
    shift_term = turned
    value = inverse * (part - jnp.where(lane < 64, mean, mean_tangent) * weight_sum)
    primal = value + shift_term + bias
    tangent = value - inverse * project * pltpu.roll(value, 64, 1)
    return jnp.where(lane < 64, primal, tangent).astype(BF16)


def kernel(
    x_any, dx_any, shift_ref, scale_ref, hw_any, bias_ref, inw_any, inb_ref, gain_ref, mid_any,
    out_ref,
    xv, dxv, hwv, inwv, part, part_in, tiles, tiles_in, block, grid, pairs, wide, acts, resid,
    midw, sums_out, sums_in,
    load_sem, mid_sem, b_send, b_recv, c_send, c_recv, g_send, g_recv, m_send, m_recv, r_send, r_recv,
):
    seq = lax.axis_index("seq")
    slab = lax.axis_index("slab")
    y = lax.rem(seq, CG)
    group = lax.div(seq, CG)
    core = lax.rem(slab, 2)
    half = lax.div(slab, 2)
    late = (y < 4).astype(jnp.int32)
    tile_group = lax.rem(group - late + GROUPS, GROUPS)
    column = lax.rem(y + 4, CG)

    loads = [
        pltpu.make_async_copy(x_any, xv, load_sem.at[0]),
        pltpu.make_async_copy(dx_any, dxv, load_sem.at[1]),
        pltpu.make_async_copy(hw_any, hwv, load_sem.at[2]),
        pltpu.make_async_copy(inw_any, inwv, load_sem.at[3]),
    ]
    for copy in loads:
        copy.start()

    barrier = pltpu.get_barrier_semaphore()
    for k in range(1, SLABS):
        pl.semaphore_signal(
            barrier, inc=1, device_id=(seq, lax.rem(slab + k, SLABS)), device_id_type=MESH
        )
    for k in range(1, CG):
        pl.semaphore_signal(
            barrier, inc=1, device_id=(group * CG + lax.rem(y + k, CG), slab), device_id_type=MESH
        )
    for k in (1, 2, 3, GROUPS - 3, GROUPS - 2, GROUPS - 1):
        pl.semaphore_signal(
            barrier, inc=1, device_id=(lax.rem(group + k, GROUPS) * CG + y, slab), device_id_type=MESH
        )

    spare = pl.multiple_of(192 - 192 * half, 64)
    midw[:, pl.ds(spare, 64), :] = jnp.zeros((27, 64, CH), BF16)
    own_rows = pl.multiple_of(half * 64 + core * SHARE, 32)
    mid_copy = pltpu.make_async_copy(mid_any, midw.at[:, pl.ds(own_rows, SHARE), :], mid_sem)
    mid_copy.start()

    loads[0].wait()
    loads[1].wait()
    loads[2].wait()
    head_partials(xv, dxv, hwv, scale_ref, shift_ref, part)

    pl.semaphore_wait(barrier, 3 + 7 + 6)

    b_copies = []
    for k in (2, 3, 1):
        b_copies.append(
            pltpu.make_async_remote_copy(
                src_ref=part,
                dst_ref=part_in.at[k - 1],
                send_sem=b_send.at[k - 1],
                recv_sem=b_recv.at[k - 1],
                device_id=(seq, lax.rem(slab + k, SLABS)),
                device_id_type=MESH,
            )
        )
        b_copies[-1].start()

    loads[3].wait()
    for par in range(2):
        for q in range(2):
            for a in range(3):
                for i in range(4):
                    for j in range(4):
                        tap_row, tap_col = (i - par, j - q)
                        cell = (i // 2) * 8 + (j // 2) * 4 + (i % 2) * 2 + j % 2
                        rows = slice(a * 256 + cell * 16, a * 256 + cell * 16 + 16)
                        if 0 <= tap_row < 3 and 0 <= tap_col < 3:
                            piece = inwv[a * 9 + tap_row * 3 + tap_col]
                        else:
                            piece = jnp.zeros((16, CH), BF16)
                        wide[par * 2 + q, rows, :] = piece

    quarter = lax.rem(y, 4)
    is_main = lax.rem(quarter, 2) == core
    row = lax.broadcasted_iota(jnp.int32, (256, TOK), 0)
    token = lax.broadcasted_iota(jnp.int32, (256, TOK), 1)
    t = row & 7
    col = 2 * (((row >> 5) + 4) & 7) - 1 + ((row >> 3) & 3)
    edge_row = jnp.where(t == 0, 5, jnp.where(t == 7, 0, -1))
    main_row = jnp.where((t == 0) | (t == 7), -1, t - 1)
    src_row = jnp.where(is_main, main_row, edge_row)
    hit = (src_row >= 0) & (col >= 0) & (col < 16) & (token == src_row * 16 + col)
    pick = jnp.where(hit, 1.0, 0.0).astype(BF16)

    for copy in b_copies:
        copy.wait_recv()
    total = part[...] + part_in[0] + part_in[1] + part_in[2]
    patches = head_finish(total, bias_ref[...])
    spread = jnp.dot(pick, patches, preferred_element_type=F32).astype(BF16)
    tiles[...] = spread.reshape(CG, 32, 128)

    c_copies = []
    for k in (4, 3, 5, 2, 6, 1, 7):
        to = lax.rem(y + k, CG)
        c_copies.append(
            pltpu.make_async_remote_copy(
                src_ref=tiles.at[to],
                dst_ref=tiles_in.at[y],
                send_sem=c_send.at[k],
                recv_sem=c_recv.at[k],
                device_id=(group * CG + to, slab),
                device_id_type=MESH,
            )
        )
        c_copies[-1].start()
    tiles_in[y] = tiles[y]

    mid_swap = pltpu.make_async_remote_copy(
        src_ref=mid_any,
        dst_ref=midw.at[:, pl.ds(own_rows, SHARE), :],
        send_sem=m_send,
        recv_sem=m_recv,
        device_id=(seq, half * 2 + 1 - core),
        device_id_type=MESH,
    )
    mid_swap.start()

    for copy in c_copies:
        copy.wait_recv()
    t32 = lax.broadcasted_iota(jnp.int32, (32, 128), 0) & 7
    for f in range(2):
        for b in range(2):
            q = 2 * b + core
            main = tiles_in[4 * f + q].astype(F32)
            above = tiles_in[4 * f + jnp.maximum(q - 1, 0)].astype(F32)
            below = tiles_in[4 * f + jnp.minimum(q + 1, 3)].astype(F32)
            value = main
            value = value + jnp.where((t32 == 0) & (q > 0), above, 0.0)
            value = value + jnp.where((t32 == 7) & (q < 3), below, 0.0)
            block[f * 2 + b] = value.astype(BF16)

    g_copies = []
    for d in (2, 1, 0):
        g_copies.append(
            pltpu.make_async_remote_copy(
                src_ref=block,
                dst_ref=grid.at[2 - d],
                send_sem=g_send.at[d],
                recv_sem=g_recv.at[d],
                device_id=(lax.rem(group + d + late, GROUPS) * CG + y, slab),
                device_id_type=MESH,
            )
        )
    g_copies[0].start()
    g_copies[1].start()

    @pl.when(y < 4)
    def _():
        g_copies[2].start()
        g_copies[2].wait()

    @pl.when(y >= 4)
    def _():
        grid[2] = block[...]

    g_copies[0].wait_recv()
    g_copies[1].wait_recv()

    lane = lanes_of((2, 8, 128))
    low = lane < 64
    for slot in range(3):
        keep = jnp.where(tile_group >= 2 - slot, 1.0, 0.0)
        for f in range(2):
            cols = []
            turned = []
            cell = grid[slot, 2 * f : 2 * f + 2].astype(F32).reshape(2, 4, 8, 128) * keep
            for w in range(4):
                value = cell[:, w]
                cols.append(value)
                turned.append(pltpu.roll(value, 64, 2))
            for kind in range(2):
                for w in range(3):
                    if kind == 0:
                        pair = jnp.where(low, cols[w], turned[w + 1])
                    else:
                        pair = jnp.where(low, turned[w], cols[w + 1])
                    below = pltpu.roll(pair, 7, 1)
                    base = (slot * 2 + f) * 96 + kind * 48 + w * 16
                    pairs[base : base + 16, 0:128] = pair.reshape(16, 128).astype(BF16)
                    pairs[base : base + 16, 128:256] = below.reshape(16, 128).astype(BF16)

    window = jnp.concatenate([pairs[0:384], pairs[96:480], pairs[192:576]], axis=1)
    bias_in = inb_ref[...].reshape(1, 1, CH)
    gain = gain_ref[...].reshape(1, 1, CH)
    first_half = half == 0
    gain_own = jnp.where(first_half, gain[..., 0:256], gain[..., 128:384])
    shape = (4, 48, 1)
    frame = lax.broadcasted_iota(jnp.int32, shape, 0)
    line = lax.broadcasted_iota(jnp.int32, shape, 1)
    s = line & 7
    b_of = (line >> 3) & 1
    w_of = line >> 4
    for par in range(2):
        for q in range(2):
            conv = jnp.dot(window, wide[par * 2 + q], preferred_element_type=F32)
            conv = conv.reshape(4, 2, 48, CH)
            feat = conv[:, 0] + bias_in
            dfeat = conv[:, 1]
            scale_inv = lax.rsqrt(jnp.mean(feat * feat, axis=-1, keepdims=True) + 1e-06)
            along = jnp.mean(feat * dfeat, axis=-1, keepdims=True)
            feat_own = jnp.where(first_half, feat[..., 0:256], feat[..., 128:384])
            dfeat_own = jnp.where(first_half, dfeat[..., 0:256], dfeat[..., 128:384])
            normed = gain_own * feat_own * scale_inv
            tang = gain_own * scale_inv * (dfeat_own - feat_own * (scale_inv * scale_inv * along))
            sig = 1.0 / (1.0 + jnp.exp(-normed))
            act = sig * (1.0 + normed * (1.0 - sig)) * tang
            out_side = (frame < 2) & (tile_group == 0)
            if q == 0:
                out_side = out_side | ((w_of == 0) & (column == 0))
            else:
                out_side = out_side | ((w_of == 2) & (column == CG - 1))
            if par == 0:
                out_side = out_side | ((s == 0) & (2 * b_of + core == 0))
            else:
                out_side = out_side | ((s == 6) & (2 * b_of + core == 3))
            act = jnp.where(out_side, 0.0, act)
            moved = pltpu.roll(act.reshape(24, 8, 256), 7, 1).reshape(4, 3, 16, 256).astype(BF16)
            act = act.reshape(4, 3, 16, 256).astype(BF16)
            for w in range(3):
                acts[par, 2 * w + q] = act[:, w]
                acts[par + 2, 2 * w + q] = moved[:, w]
            keep = dfeat[2:4].reshape(2, 3, 2, 8, CH)
            keep = jnp.where(first_half, keep[:, :, 0], keep[:, :, 1])
            if par == 0:
                keep = pltpu.roll(keep.reshape(6, 8, CH), 7, 1).reshape(2, 3, 8, CH)
            for w in range(3):
                place = 2 * w + q - 1
                if 0 <= place < 4:
                    resid[1 - par, place] = keep[:, w]

    mid_copy.wait()
    mid_swap.wait()
    acc = jnp.zeros((256, CH), F32)
    for a in range(3):
        for b in range(3):
            for c in range(3):
                taken = acts[b : b + 2, c : c + 4, a : a + 2].reshape(256, 256)
                acc = acc + jnp.dot(taken, midw[a * 9 + b * 3 + c], preferred_element_type=F32)
    acc = acc.reshape(16, 2, 8, CH)
    mine = jnp.where(first_half, acc[:, 0], acc[:, 1])
    other = jnp.where(first_half, acc[:, 1], acc[:, 0])
    sums_out[...] = other.reshape(128, CH).astype(BF16)
    swap = pltpu.make_async_remote_copy(
        src_ref=sums_out,
        dst_ref=sums_in,
        send_sem=r_send,
        recv_sem=r_recv,
        device_id=(seq, (1 - half) * 2 + core),
        device_id_type=MESH,
    )
    swap.start()
    swap.wait_recv()
    final = mine.reshape(128, CH) + sums_in[...].astype(F32) + resid[...].reshape(128, CH)
    row = lax.broadcasted_iota(jnp.int32, (TOK, 128), 0)
    src = lax.broadcasted_iota(jnp.int32, (TOK, 128), 1)
    upper = row >= 48
    inner = jnp.where(upper, row - 48, row)
    want = ((inner >> 2) & 1) * 64 + (inner & 3) * 16 + jnp.where(upper, 8, 0) + (inner >> 3)
    order = jnp.where(src == want, 1.0, 0.0).astype(BF16)
    out_ref[...] = jnp.dot(order, final.astype(BF16), preferred_element_type=F32).astype(BF16)

    for copy in b_copies + c_copies + g_copies[0:2]:
        copy.wait_send()
    swap.wait_send()


def shards(hidden, tangent, mod_shift, mod_scale, head_weight, head_bias, in_weight, in_bias, norm_gain, mid_weight):
    any_spec = pl.BlockSpec(memory_space=pl.ANY)
    vmem = pl.BlockSpec(memory_space=pltpu.VMEM)
    bias = jnp.pad(head_bias, (0, 64)).reshape(1, 128)
    dma = pltpu.SemaphoreType.DMA
    out = pl.pallas_call(
        kernel,
        out_shape=jax.ShapeDtypeStruct((TOK, CH), BF16),
        in_specs=[any_spec, any_spec, vmem, vmem, any_spec, vmem, any_spec, vmem, vmem, any_spec],
        out_specs=vmem,
        scratch_shapes=[
            pltpu.VMEM((TOK, DS), BF16),
            pltpu.VMEM((TOK, DS), BF16),
            pltpu.VMEM((64, DS), BF16),
            pltpu.VMEM((27, 16, CH), BF16),
            pltpu.VMEM((TOK + 16, 128), F32),
            pltpu.VMEM((3, TOK + 16, 128), F32),
            pltpu.VMEM((CG, 32, 128), BF16),
            pltpu.VMEM((CG, 32, 128), BF16),
            pltpu.VMEM((4, 32, 128), BF16),
            pltpu.VMEM((3, 4, 32, 128), BF16),
            pltpu.VMEM((576, 256), BF16),
            pltpu.VMEM((4, 768, CH), BF16),
            pltpu.VMEM((4, 6, 4, 16, 256), BF16),
            pltpu.VMEM((2, 4, 2, 8, CH), F32),
            pltpu.VMEM((27, 256, CH), BF16),
            pltpu.VMEM((128, CH), BF16),
            pltpu.VMEM((128, CH), BF16),
            dma((4,)),
            dma,
            dma((3,)),
            dma((3,)),
            dma((CG,)),
            dma((CG,)),
            dma((3,)),
            dma((3,)),
            dma,
            dma,
            dma,
            dma,
        ],
        compiler_params=pltpu.CompilerParams(collective_id=0, has_side_effects=True),
        name="decode",
    )(
        hidden,
        tangent,
        mod_shift,
        mod_scale,
        head_weight,
        bias,
        in_weight.reshape(27, 16, CH),
        in_bias,
        norm_gain,
        mid_weight.reshape(27, SHARE, CH),
    )
    return out.reshape(1, 2, 12, 4, CH)


def solution(mesh):
    return jax.shard_map(
        shards,
        mesh=mesh,
        in_specs=(
            P("seq", "slab"),
            P("seq", "slab"),
            P("slab"),
            P("slab"),
            P(None, "slab"),
            P(),
            P(),
            P(),
            P(),
            P(None, None, None, "slab", None),
        ),
        out_specs=P("seq", None, "slab", None, None),
        check_vma=False,
    )
```

time: 207 us -> 41.7 us (0.20)
  the two profiles are of different devices: /device:TPU:1 before, /device:TPU:16 now
where the time goes in v1:
time: 41.7 us; the launch traced here: 41.5 us
  Pallas kernels  38.8 us (93%)
  local copies, waits for them, and re-layouts  2.71 us (6%)
    pallas_call x1, Pallas kernels, shards(): pl.pallas_call(kernel, out_shape=jax.ShapeDtypeStruct((TOK, CH), BF16), i...  38.8 us
    reshape x1, local copies, waits for them, and re-layouts, shards(): return out.reshape(1, 2, 12, 4, CH)  1.54 us
    reshape x1, local copies, waits for them, and re-layouts, shards(): bias = jnp.pad(head_bias, (0, 64)).reshape(1, 128)  1.17 us

profile of v1, /device:TPU:16, one launch (start us, length us, event | category | flops | bytes accessed | tf_op | source)
XLA Modules:
  0.0 41.5 jit_solution(495247420856820747)
XLA Ops:
  0.0 1.2 %pad_bitcast_fusion.bias_ref = f32[1,128]{1,0:T(1,128)} fusion(f32[64]{0:T(128)} %param.15), kind=kLoop, calls=%fused_computation | loop fusion | bytes 768 | tf_op jit(solution)/shard_map/reshape | solution.py:369
  1.2 38.8 %decode.1 = bf16[96,384]{1,0:T(8,128)(2,1)} custom-call(bf16[96,1280]{1,0:T(8,128)(2,1)} %x_any.1, bf16[96,1280]{1,0:T(8,128)(2,1)} %dx_any.1, f32[1280]{0:T(1024)} %shift_ref.1, f32[1280]{0:T(1024)} %scale_ref.1, bf16[64,1280]{1,0:T(8,128)(2,1)} %hw_any.1, f32[1,128]{1,0:T(1,128)} %pad_bitcast_fusion.bias_ref, bf16[27,16,384]{2,1,0:T(8,128)(2,1)} %bitcast.5, ...), custom_call_target="tpu_custom_call" | custom-call | tf_op jit(solution)/shard_map/decode/pallas_call | solution.py:371
  40.0 1.5 %reshape.15 = bf16[1,2,12,4,384]{4,3,2,1,0:T(4,128)(2,1)} reshape(bf16[96,384]{1,0:T(8,128)(2,1)} %decode.1) | data formatting | bytes 147456 | tf_op jit(solution)/shard_map/reshape | solution.py:421

commit v2 on v1

--- a/solution.py
+++ b/solution.py
@@ -61,13 +61,16 @@
     lane1 = lanes_of((8, 128))
     ones_row = jnp.broadcast_to(prod[2 * TOK : 2 * TOK + 1], (8, 128))
     shift_row = jnp.broadcast_to(shifted[1:2] + shifted[2:3] + shifted[3:4], (8, 128))
-    send[0:TOK, :] = jnp.where(lane < 64, prod[0:TOK], prod[TOK : 2 * TOK])
+    value = jnp.where(lane < 64, prod[0:TOK], prod[TOK : 2 * TOK])
+    send[0:64, :] = value[16:80]
+    send[64:80, :] = value[0:16]
+    send[80:96, :] = value[80:96]
     send[TOK : TOK + 8, :] = jnp.transpose(moments)[0:8]
     send[TOK + 8 : TOK + 16, :] = jnp.where(lane1 < 64, ones_row, shift_row)
 
 
 def head_finish(total, bias):
-    part = total[0:TOK]
+    part = jnp.concatenate([total[64:80], total[0:64], total[80:96]], axis=0)
     moments = jnp.concatenate([total[TOK : TOK + 8], jnp.zeros((120, 128), F32)], axis=0)
     moments = jnp.transpose(moments)[0:TOK]
     const = total[TOK + 8 : TOK + 9]
@@ -88,11 +91,11 @@
 
 
 def kernel(
-    x_any, dx_any, shift_ref, scale_ref, hw_any, bias_ref, inw_any, inb_ref, gain_ref, mid_any,
+    x_any, dx_any, shift_any, scale_any, hw_any, bias_any, inw_any, inb_any, gain_any, mid_any,
     out_ref,
-    xv, dxv, hwv, inwv, part, part_in, tiles, tiles_in, block, grid, pairs, wide, acts, resid,
+    xv, dxv, hwv, inwv, shift_ref, scale_ref, bias_ref, inb_ref, gain_ref, part, part_in, tiles, tiles_in, block, grid, pairs, wide, acts, resid,
     midw, sums_out, sums_in,
-    load_sem, mid_sem, b_send, b_recv, c_send, c_recv, g_send, g_recv, m_send, m_recv, r_send, r_recv,
+    near_sem, far_sem, load_sem, mid_sem, b_send, b_recv, c_send, c_recv, g_send, g_recv, m_send, m_recv, r_send, r_recv,
 ):
     seq = lax.axis_index("seq")
     slab = lax.axis_index("slab")
@@ -104,57 +107,77 @@
     tile_group = lax.rem(group - late + GROUPS, GROUPS)
     column = lax.rem(y + 4, CG)
 
-    loads = [
-        pltpu.make_async_copy(x_any, xv, load_sem.at[0]),
-        pltpu.make_async_copy(dx_any, dxv, load_sem.at[1]),
-        pltpu.make_async_copy(hw_any, hwv, load_sem.at[2]),
-        pltpu.make_async_copy(inw_any, inwv, load_sem.at[3]),
-    ]
+    part_in[:, 0:64, :] = jnp.zeros((3, 64, 128), F32)
+    barrier = pltpu.get_barrier_semaphore()
+    z_hi = lax.div(group, 4)
+    x = lax.rem(group, 4)
+
+    def place(z_to, x_to, y_to):
+        return (lax.rem(z_to, 4) * 4 + lax.rem(x_to, 4)) * CG + lax.rem(y_to, CG)
+
+    beside_x = [(place(z_hi, x + k, y), slab) for k in (1, 3)]
+    beside_z = [(place(z_hi + k, x, y), slab) for k in (1, 3)]
+    beside_y = [(place(z_hi, x, y + k), slab) for k in (2, 6, 1, 7)]
+    in_slab = [(seq, lax.rem(slab + k, SLABS)) for k in range(1, SLABS)]
+    for device in beside_z + beside_y + beside_x + in_slab:
+        pl.semaphore_signal(barrier, inc=1, device_id=device, device_id_type=MESH)
+
+    moves = (
+        (x_any, xv),
+        (dx_any, dxv),
+        (hw_any, hwv),
+        (scale_any, scale_ref),
+        (shift_any, shift_ref),
+        (inw_any, inwv),
+        (bias_any, bias_ref),
+        (inb_any, inb_ref),
+        (gain_any, gain_ref),
+    )
+    loads = [pltpu.make_async_copy(src, dst, load_sem.at[k]) for k, (src, dst) in enumerate(moves)]
     for copy in loads:
         copy.start()
-
-    barrier = pltpu.get_barrier_semaphore()
-    for k in range(1, SLABS):
-        pl.semaphore_signal(
-            barrier, inc=1, device_id=(seq, lax.rem(slab + k, SLABS)), device_id_type=MESH
-        )
-    for k in range(1, CG):
-        pl.semaphore_signal(
-            barrier, inc=1, device_id=(group * CG + lax.rem(y + k, CG), slab), device_id_type=MESH
-        )
-    for k in (1, 2, 3, GROUPS - 3, GROUPS - 2, GROUPS - 1):
-        pl.semaphore_signal(
-            barrier, inc=1, device_id=(lax.rem(group + k, GROUPS) * CG + y, slab), device_id_type=MESH
-        )
 
     spare = pl.multiple_of(192 - 192 * half, 64)
     midw[:, pl.ds(spare, 64), :] = jnp.zeros((27, 64, CH), BF16)
     own_rows = pl.multiple_of(half * 64 + core * SHARE, 32)
     mid_copy = pltpu.make_async_copy(mid_any, midw.at[:, pl.ds(own_rows, SHARE), :], mid_sem)
+
+    for copy in loads[0:5]:
+        copy.wait()
     mid_copy.start()
-
-    loads[0].wait()
-    loads[1].wait()
-    loads[2].wait()
     head_partials(xv, dxv, hwv, scale_ref, shift_ref, part)
 
-    pl.semaphore_wait(barrier, 3 + 7 + 6)
-
-    b_copies = []
+    pl.semaphore_wait(barrier, 11)
+    for device in beside_z + beside_y[0:2] + beside_x:
+        pl.semaphore_signal(near_sem, inc=1, device_id=device, device_id_type=MESH)
+
+    quarter = lax.rem(y, 4)
+    main_core = lax.rem(quarter, 2)
+    is_main = main_core == core
+
+    def slab_copy(k, start):
+        return pltpu.make_async_remote_copy(
+            src_ref=part.at[start : TOK + 16],
+            dst_ref=part_in.at[k - 1, start : TOK + 16],
+            send_sem=b_send.at[k - 1],
+            recv_sem=b_recv.at[k - 1],
+            device_id=(seq, lax.rem(slab + k, SLABS)),
+            device_id_type=MESH,
+        )
+
     for k in (2, 3, 1):
-        b_copies.append(
-            pltpu.make_async_remote_copy(
-                src_ref=part,
-                dst_ref=part_in.at[k - 1],
-                send_sem=b_send.at[k - 1],
-                recv_sem=b_recv.at[k - 1],
-                device_id=(seq, lax.rem(slab + k, SLABS)),
-                device_id_type=MESH,
-            )
-        )
-        b_copies[-1].start()
-
-    loads[3].wait()
+        to_main = lax.rem(slab + k, 2) == main_core
+
+        @pl.when(to_main)
+        def _():
+            slab_copy(k, 0).start()
+
+        @pl.when(jnp.logical_not(to_main))
+        def _():
+            slab_copy(k, 64).start()
+
+    for copy in loads[5:]:
+        copy.wait()
     for par in range(2):
         for q in range(2):
             for a in range(3):
@@ -169,8 +192,6 @@
                             piece = jnp.zeros((16, CH), BF16)
                         wide[par * 2 + q, rows, :] = piece
 
-    quarter = lax.rem(y, 4)
-    is_main = lax.rem(quarter, 2) == core
     row = lax.broadcasted_iota(jnp.int32, (256, TOK), 0)
     token = lax.broadcasted_iota(jnp.int32, (256, TOK), 1)
     t = row & 7
@@ -181,10 +202,23 @@
     hit = (src_row >= 0) & (col >= 0) & (col < 16) & (token == src_row * 16 + col)
     pick = jnp.where(hit, 1.0, 0.0).astype(BF16)
 
-    for copy in b_copies:
-        copy.wait_recv()
+    pl.semaphore_wait(near_sem, 6)
+    for device in beside_x:
+        pl.semaphore_signal(far_sem, inc=1, device_id=device, device_id_type=MESH)
+
+    @pl.when(is_main)
+    def _():
+        for k in (1, 3, 2):
+            slab_copy(k, 0).wait_recv()
+
+    @pl.when(jnp.logical_not(is_main))
+    def _():
+        for k in (1, 3, 2):
+            slab_copy(k, 64).wait_recv()
+
     total = part[...] + part_in[0] + part_in[1] + part_in[2]
-    patches = head_finish(total, bias_ref[...])
+    bias = bias_ref[...].reshape(1, 64)
+    patches = head_finish(total, jnp.concatenate([bias, bias], axis=1))
     spread = jnp.dot(pick, patches, preferred_element_type=F32).astype(BF16)
     tiles[...] = spread.reshape(CG, 32, 128)
 
@@ -240,6 +274,7 @@
                 device_id_type=MESH,
             )
         )
+    pl.semaphore_wait(far_sem, 2)
     g_copies[0].start()
     g_copies[1].start()
 
@@ -313,11 +348,13 @@
             else:
                 out_side = out_side | ((s == 6) & (2 * b_of + core == 3))
             act = jnp.where(out_side, 0.0, act)
-            moved = pltpu.roll(act.reshape(24, 8, 256), 7, 1).reshape(4, 3, 16, 256).astype(BF16)
-            act = act.reshape(4, 3, 16, 256).astype(BF16)
-            for w in range(3):
-                acts[par, 2 * w + q] = act[:, w]
-                acts[par + 2, 2 * w + q] = moved[:, w]
+            moved = pltpu.roll(act.reshape(24, 8, 256), 7, 1).reshape(4, 3, 2, 8, 256)
+            act = act.reshape(4, 3, 2, 8, 256)
+            for plane, value in ((par, act), (par + 2, moved)):
+                for a in range(3):
+                    both = jnp.concatenate([value[a], value[a + 1]], axis=2).astype(BF16)
+                    for w in range(3):
+                        acts[:, plane, 2 * w + q, a] = both[w]
             keep = dfeat[2:4].reshape(2, 3, 2, 8, CH)
             keep = jnp.where(first_half, keep[:, :, 0], keep[:, :, 1])
             if par == 0:
@@ -329,16 +366,25 @@
 
     mid_copy.wait()
     mid_swap.wait()
-    acc = jnp.zeros((256, CH), F32)
-    for a in range(3):
-        for b in range(3):
-            for c in range(3):
-                taken = acts[b : b + 2, c : c + 4, a : a + 2].reshape(256, 256)
-                acc = acc + jnp.dot(taken, midw[a * 9 + b * 3 + c], preferred_element_type=F32)
-    acc = acc.reshape(16, 2, 8, CH)
-    mine = jnp.where(first_half, acc[:, 0], acc[:, 1])
-    other = jnp.where(first_half, acc[:, 1], acc[:, 0])
-    sums_out[...] = other.reshape(128, CH).astype(BF16)
+
+    row = lax.broadcasted_iota(jnp.int32, (TOK, 128), 0)
+    src = lax.broadcasted_iota(jnp.int32, (TOK, 128), 1)
+    upper = row >= 48
+    inner = jnp.where(upper, row - 48, row)
+    want = ((inner >> 2) & 1) * 64 + (inner & 3) * 16 + jnp.where(upper, 8, 0) + (inner >> 3)
+    order = jnp.where(src == want, 1.0, 0.0).astype(BF16)
+
+    def mid_conv(block_of):
+        acc = jnp.zeros((128, CH), F32)
+        for a in range(3):
+            for b in range(3):
+                for c in range(3):
+                    taken = acts[block_of, b : b + 2, c : c + 4, a].reshape(128, 256)
+                    acc = acc + jnp.dot(taken, midw[a * 9 + b * 3 + c], preferred_element_type=F32)
+        return acc
+
+    other = mid_conv(1 - half).astype(BF16)
+    sums_out[...] = jnp.dot(order, other, preferred_element_type=F32).astype(BF16)
     swap = pltpu.make_async_remote_copy(
         src_ref=sums_out,
         dst_ref=sums_in,
@@ -348,17 +394,25 @@
         device_id_type=MESH,
     )
     swap.start()
+    mine = mid_conv(half) + resid[...].reshape(128, CH)
+    high = mine.astype(BF16)
+    low_part = (mine - high.astype(F32)).astype(BF16)
+    mine = jnp.dot(order, high, preferred_element_type=F32) + jnp.dot(order, low_part, preferred_element_type=F32)
     swap.wait_recv()
-    final = mine.reshape(128, CH) + sums_in[...].astype(F32) + resid[...].reshape(128, CH)
-    row = lax.broadcasted_iota(jnp.int32, (TOK, 128), 0)
-    src = lax.broadcasted_iota(jnp.int32, (TOK, 128), 1)
-    upper = row >= 48
-    inner = jnp.where(upper, row - 48, row)
-    want = ((inner >> 2) & 1) * 64 + (inner & 3) * 16 + jnp.where(upper, 8, 0) + (inner >> 3)
-    order = jnp.where(src == want, 1.0, 0.0).astype(BF16)
-    out_ref[...] = jnp.dot(order, final.astype(BF16), preferred_element_type=F32).astype(BF16)
-
-    for copy in b_copies + c_copies + g_copies[0:2]:
+    out_ref[...] = (mine + sums_in[...].astype(F32)).astype(BF16)
+
+    for k in (1, 2, 3):
+        to_main = lax.rem(slab + k, 2) == main_core
+
+        @pl.when(to_main)
+        def _():
+            slab_copy(k, 0).wait_send()
+
+        @pl.when(jnp.logical_not(to_main))
+        def _():
+            slab_copy(k, 64).wait_send()
+
+    for copy in c_copies + g_copies[0:2]:
         copy.wait_send()
     swap.wait_send()
 
@@ -366,18 +420,22 @@
 def shards(hidden, tangent, mod_shift, mod_scale, head_weight, head_bias, in_weight, in_bias, norm_gain, mid_weight):
     any_spec = pl.BlockSpec(memory_space=pl.ANY)
     vmem = pl.BlockSpec(memory_space=pltpu.VMEM)
-    bias = jnp.pad(head_bias, (0, 64)).reshape(1, 128)
     dma = pltpu.SemaphoreType.DMA
     out = pl.pallas_call(
         kernel,
         out_shape=jax.ShapeDtypeStruct((TOK, CH), BF16),
-        in_specs=[any_spec, any_spec, vmem, vmem, any_spec, vmem, any_spec, vmem, vmem, any_spec],
+        in_specs=[any_spec] * 10,
         out_specs=vmem,
         scratch_shapes=[
             pltpu.VMEM((TOK, DS), BF16),
             pltpu.VMEM((TOK, DS), BF16),
             pltpu.VMEM((64, DS), BF16),
             pltpu.VMEM((27, 16, CH), BF16),
+            pltpu.VMEM((DS,), F32),
+            pltpu.VMEM((DS,), F32),
+            pltpu.VMEM((64,), F32),
+            pltpu.VMEM((CH,), F32),
+            pltpu.VMEM((CH,), F32),
             pltpu.VMEM((TOK + 16, 128), F32),
             pltpu.VMEM((3, TOK + 16, 128), F32),
             pltpu.VMEM((CG, 32, 128), BF16),
@@ -386,12 +444,14 @@
             pltpu.VMEM((3, 4, 32, 128), BF16),
             pltpu.VMEM((576, 256), BF16),
             pltpu.VMEM((4, 768, CH), BF16),
-            pltpu.VMEM((4, 6, 4, 16, 256), BF16),
+            pltpu.VMEM((2, 4, 6, 3, 16, 256), BF16),
             pltpu.VMEM((2, 4, 2, 8, CH), F32),
             pltpu.VMEM((27, 256, CH), BF16),
-            pltpu.VMEM((128, CH), BF16),
-            pltpu.VMEM((128, CH), BF16),
-            dma((4,)),
+            pltpu.VMEM((TOK, CH), BF16),
+            pltpu.VMEM((TOK, CH), BF16),
+            pltpu.SemaphoreType.REGULAR,
+            pltpu.SemaphoreType.REGULAR,
+            dma((9,)),
             dma,
             dma((3,)),
             dma((3,)),
@@ -412,7 +472,7 @@
         mod_shift,
         mod_scale,
         head_weight,
-        bias,
+        head_bias,
         in_weight.reshape(27, 16, CH),
         in_bias,
         norm_gain,

time: 41.7 us -> 37.6 us (0.902)
  the two profiles are of different devices: /device:TPU:16 before, /device:TPU:8 now
where the time goes in v2:
time: 37.6 us; the launch traced here: 37.5 us
  Pallas kernels  35.9 us (95%)
  local copies, waits for them, and re-layouts  1.54 us (4%)
    pallas_call x1, Pallas kernels, shards(): pl.pallas_call(kernel, out_shape=jax.ShapeDtypeStruct((TOK, CH), BF16), i...  35.9 us
    reshape x1, local copies, waits for them, and re-layouts, shards(): return out.reshape(1, 2, 12, 4, CH)  1.54 us

profile of v2, /device:TPU:8, one launch (start us, length us, event | category | flops | bytes accessed | tf_op | source)
XLA Modules:
  0.0 37.5 jit_solution(9393878079056781278)
XLA Ops:
  0.0 35.9 %decode.1 = bf16[96,384]{1,0:T(8,128)(2,1)} custom-call(bf16[96,1280]{1,0:T(8,128)(2,1)} %x_any.1, bf16[96,1280]{1,0:T(8,128)(2,1)} %dx_any.1, f32[1280]{0:T(1024)} %shift_any.1, f32[1280]{0:T(1024)} %scale_any.1, bf16[64,1280]{1,0:T(8,128)(2,1)} %hw_any.1, f32[64]{0:T(128)} %bias_any.1, bf16[27,16,384]{2,1,0:T(8,128)(2,1)} %bitcast.3, f32[384]{0:T(512)} %inb_any.1, ...), custom_call_target="tpu_custom_call" | custom-call | tf_op jit(solution)/shard_map/decode/pallas_call | solution.py:424
  35.9 1.5 %reshape.11 = bf16[1,2,12,4,384]{4,3,2,1,0:T(4,128)(2,1)} reshape(bf16[96,384]{1,0:T(8,128)(2,1)} %decode.1) | data formatting | bytes 147456 | tf_op jit(solution)/shard_map/reshape | solution.py:481

commit v3 on v2

--- a/solution.py
+++ b/solution.py
@@ -23,12 +23,12 @@
     return lax.broadcasted_iota(jnp.int32, shape, len(shape) - 1)
 
 
-def head_partials(xv, dxv, hwv, scale_ref, shift_ref, send):
+def head_partials(xv, dxv, hwv, scale_ref, shift_ref, part, sums):
     x = xv[...]
     dx = dxv[...]
     xf = x.astype(F32)
     dxf = dx.astype(F32)
-    sums = [
+    values = [
         jnp.sum(xf, axis=1, keepdims=True),
         jnp.sum(xf * xf, axis=1, keepdims=True),
         jnp.sum(dxf, axis=1, keepdims=True),
@@ -36,7 +36,7 @@
     ]
     lane = lanes_of((TOK, 128))
     moments = jnp.zeros((TOK, 128), F32)
-    for k, value in enumerate(sums):
+    for k, value in enumerate(values):
         moments = jnp.where(lane == k, value, moments)
     moments = jnp.concatenate([moments, jnp.zeros((128 - TOK, 128), F32)], axis=0)
     w = hwv[...]
@@ -58,33 +58,43 @@
     prod = prod + pltpu.roll(prod, 64, 1)
     twice = jnp.concatenate([w, w], axis=0)
     shifted = lax.dot_general(extra, twice, NT, preferred_element_type=F32)
+    weight_sum = prod[2 * TOK : 2 * TOK + 1]
+    shift_sum = shifted[1:2] + shifted[2:3] + shifted[3:4]
+    value = jnp.where(lane < 64, prod[0:TOK], prod[TOK : 2 * TOK])
+    value = value - jnp.where(lane < 64, values[0] / DS, values[2] / DS) * weight_sum
+    send = value.astype(BF16)
+    part[0:64, :] = send[16:80]
+    part[64:80, :] = send[0:16]
+    part[80:96, :] = send[80:96]
+    const = jnp.where(lanes_of((1, 128)) < 64, weight_sum, shift_sum)
+    row8 = lax.broadcasted_iota(jnp.int32, (8, 128), 0)
+    sums[...] = jnp.where(row8 == 4, const, jnp.transpose(moments)[0:8])
+    return value
+
+
+def head_finish(own, part_in, sums, bias):
+    moments = jnp.concatenate([sums, jnp.zeros((96, 128), F32)], axis=0)
+    moments = jnp.transpose(moments)[0:TOK]
+    total = moments[:, 0:8] + moments[:, 8:16] + moments[:, 16:24] + moments[:, 24:32]
+    lane = lanes_of((TOK, 128))
     lane1 = lanes_of((8, 128))
-    ones_row = jnp.broadcast_to(prod[2 * TOK : 2 * TOK + 1], (8, 128))
-    shift_row = jnp.broadcast_to(shifted[1:2] + shifted[2:3] + shifted[3:4], (8, 128))
-    value = jnp.where(lane < 64, prod[0:TOK], prod[TOK : 2 * TOK])
-    send[0:64, :] = value[16:80]
-    send[64:80, :] = value[0:16]
-    send[80:96, :] = value[80:96]
-    send[TOK : TOK + 8, :] = jnp.transpose(moments)[0:8]
-    send[TOK + 8 : TOK + 16, :] = jnp.where(lane1 < 64, ones_row, shift_row)
-
-
-def head_finish(total, bias):
-    part = jnp.concatenate([total[64:80], total[0:64], total[80:96]], axis=0)
-    moments = jnp.concatenate([total[TOK : TOK + 8], jnp.zeros((120, 128), F32)], axis=0)
-    moments = jnp.transpose(moments)[0:TOK]
-    const = total[TOK + 8 : TOK + 9]
-    mean = moments[:, 0:1] / D
-    variance = moments[:, 1:2] / D - mean * mean
+    mean = total[:, 0:1] / D
+    mean_tangent = total[:, 2:3] / D
+    received = part_in[0].astype(F32) + part_in[1].astype(F32) + part_in[2].astype(F32)
+    part = own + jnp.concatenate([received[64:80], received[0:64], received[80:96]], axis=0)
+    shift_term = jnp.zeros((1, 128), F32)
+    for k in range(4):
+        const = jnp.broadcast_to(sums[8 * k + 4 : 8 * k + 5], (8, 128))
+        turned = pltpu.roll(const, 64, 1)
+        weight_sum = jnp.where(lane1 < 64, const, turned)[0:1]
+        shift_term = shift_term + turned[0:1]
+        off = moments[:, 8 * k : 8 * k + 1] / DS - mean
+        off_tangent = moments[:, 8 * k + 2 : 8 * k + 3] / DS - mean_tangent
+        part = part + jnp.where(lane < 64, off, off_tangent) * weight_sum
+    variance = total[:, 1:2] / D - mean * mean
     inverse = lax.rsqrt(variance + 1e-06)
-    mean_tangent = moments[:, 2:3] / D
-    project = inverse * (moments[:, 3:4] / D - mean * mean_tangent)
-    lane = lanes_of((TOK, 128))
-    lane1 = lanes_of((1, 128))
-    turned = pltpu.roll(jnp.broadcast_to(const, (8, 128)), 64, 1)[0:1]
-    weight_sum = jnp.where(lane1 < 64, const, turned)
-    shift_term = turned
-    value = inverse * (part - jnp.where(lane < 64, mean, mean_tangent) * weight_sum)
+    project = inverse * (total[:, 3:4] / D - mean * mean_tangent)
+    value = inverse * part
     primal = value + shift_term + bias
     tangent = value - inverse * project * pltpu.roll(value, 64, 1)
     return jnp.where(lane < 64, primal, tangent).astype(BF16)
@@ -93,9 +103,9 @@
 def kernel(
     x_any, dx_any, shift_any, scale_any, hw_any, bias_any, inw_any, inb_any, gain_any, mid_any,
     out_ref,
-    xv, dxv, hwv, inwv, shift_ref, scale_ref, bias_ref, inb_ref, gain_ref, part, part_in, tiles, tiles_in, block, grid, pairs, wide, acts, resid,
+    xv, dxv, hwv, inwv, shift_ref, scale_ref, bias_ref, inb_ref, gain_ref, part, part_in, sums, sums_row_in, tiles, tiles_in, block, grid, pairs, wide, acts, resid,
     midw, sums_out, sums_in,
-    near_sem, far_sem, load_sem, mid_sem, b_send, b_recv, c_send, c_recv, g_send, g_recv, m_send, m_recv, r_send, r_recv,
+    near_sem, far_sem, load_sem, mid_sem, b_send, b_recv, x_send, x_recv, c_send, c_recv, g_send, g_recv, m_send, m_recv, r_send, r_recv,
 ):
     seq = lax.axis_index("seq")
     slab = lax.axis_index("slab")
@@ -107,7 +117,7 @@
     tile_group = lax.rem(group - late + GROUPS, GROUPS)
     column = lax.rem(y + 4, CG)
 
-    part_in[:, 0:64, :] = jnp.zeros((3, 64, 128), F32)
+    part_in[:, 0:64, :] = jnp.zeros((3, 64, 128), BF16)
     barrier = pltpu.get_barrier_semaphore()
     z_hi = lax.div(group, 4)
     x = lax.rem(group, 4)
@@ -123,8 +133,10 @@
         pl.semaphore_signal(barrier, inc=1, device_id=device, device_id_type=MESH)
 
     moves = (
-        (x_any, xv),
-        (dx_any, dxv),
+        (x_any.at[0:48], xv.at[0:48]),
+        (x_any.at[48:96], xv.at[48:96]),
+        (dx_any.at[0:48], dxv.at[0:48]),
+        (dx_any.at[48:96], dxv.at[48:96]),
         (hw_any, hwv),
         (scale_any, scale_ref),
         (shift_any, shift_ref),
@@ -134,7 +146,7 @@
         (gain_any, gain_ref),
     )
     loads = [pltpu.make_async_copy(src, dst, load_sem.at[k]) for k, (src, dst) in enumerate(moves)]
-    for copy in loads:
+    for copy in loads[0:7]:
         copy.start()
 
     spare = pl.multiple_of(192 - 192 * half, 64)
@@ -142,31 +154,45 @@
     own_rows = pl.multiple_of(half * 64 + core * SHARE, 32)
     mid_copy = pltpu.make_async_copy(mid_any, midw.at[:, pl.ds(own_rows, SHARE), :], mid_sem)
 
-    for copy in loads[0:5]:
-        copy.wait()
-    mid_copy.start()
-    head_partials(xv, dxv, hwv, scale_ref, shift_ref, part)
-
     pl.semaphore_wait(barrier, 11)
     for device in beside_z + beside_y[0:2] + beside_x:
         pl.semaphore_signal(near_sem, inc=1, device_id=device, device_id_type=MESH)
 
+    for copy in loads[0:7]:
+        copy.wait()
+    for copy in loads[7:]:
+        copy.start()
+    mid_copy.start()
+    own = head_partials(xv, dxv, hwv, scale_ref, shift_ref, part, sums)
+
     quarter = lax.rem(y, 4)
     main_core = lax.rem(quarter, 2)
     is_main = main_core == core
 
     def slab_copy(k, start):
         return pltpu.make_async_remote_copy(
-            src_ref=part.at[start : TOK + 16],
-            dst_ref=part_in.at[k - 1, start : TOK + 16],
+            src_ref=part.at[start:TOK],
+            dst_ref=part_in.at[k - 1, start:TOK],
             send_sem=b_send.at[k - 1],
             recv_sem=b_recv.at[k - 1],
             device_id=(seq, lax.rem(slab + k, SLABS)),
             device_id_type=MESH,
         )
 
+    sum_copies = []
     for k in (2, 3, 1):
         to_main = lax.rem(slab + k, 2) == main_core
+        sum_copies.append(
+            pltpu.make_async_remote_copy(
+                src_ref=sums,
+                dst_ref=sums_row_in.at[k - 1],
+                send_sem=x_send.at[k - 1],
+                recv_sem=x_recv.at[k - 1],
+                device_id=(seq, lax.rem(slab + k, SLABS)),
+                device_id_type=MESH,
+            )
+        )
+        sum_copies[-1].start()
 
         @pl.when(to_main)
         def _():
@@ -176,7 +202,66 @@
         def _():
             slab_copy(k, 64).start()
 
-    for copy in loads[5:]:
+    row = lax.broadcasted_iota(jnp.int32, (256, TOK), 0)
+    token = lax.broadcasted_iota(jnp.int32, (256, TOK), 1)
+    line = row & 31
+    t = line & 7
+    main_row = jnp.where((t == 0) | (t == 7), -1, t - 1)
+    edge_row = jnp.where(line < 8, jnp.where((line & 1) == 0, 5, 0), -1)
+    src_row = jnp.where(is_main, main_row, edge_row)
+    col = 2 * (((row >> 5) + 4) & 7) - 1 + jnp.where(is_main, line >> 3, line >> 1)
+    hit = (src_row >= 0) & (col >= 0) & (col < 16) & (token == src_row * 16 + col)
+    pick = jnp.where(hit, 1.0, 0.0).astype(BF16)
+
+    @pl.when(is_main)
+    def _():
+        for k in (1, 3, 2):
+            slab_copy(k, 0).wait_recv()
+
+    @pl.when(jnp.logical_not(is_main))
+    def _():
+        for k in (1, 3, 2):
+            slab_copy(k, 64).wait_recv()
+
+    for copy in sum_copies:
+        copy.wait_recv()
+    all_sums = jnp.concatenate([sums[...], sums_row_in[0], sums_row_in[1], sums_row_in[2]], axis=0)
+    loads[8].wait()
+    bias = bias_ref[...].reshape(1, 64)
+    patches = head_finish(own, part_in, all_sums, jnp.concatenate([bias, bias], axis=1))
+    spread = jnp.dot(pick, patches, preferred_element_type=F32).astype(BF16)
+    tiles[...] = spread.reshape(CG, 32, 128)
+
+    pl.semaphore_wait(near_sem, 6)
+    for device in beside_x:
+        pl.semaphore_signal(far_sem, inc=1, device_id=device, device_id_type=MESH)
+
+    def y_copy(k, rows):
+        to = lax.rem(y + k, CG)
+        return pltpu.make_async_remote_copy(
+            src_ref=tiles.at[to, 0:rows],
+            dst_ref=tiles_in.at[y, 0:rows],
+            send_sem=c_send.at[k],
+            recv_sem=c_recv.at[k],
+            device_id=(group * CG + to, slab),
+            device_id_type=MESH,
+        )
+
+    steps = (4, 3, 5, 2, 6, 1, 7)
+
+    @pl.when(is_main)
+    def _():
+        for k in steps:
+            y_copy(k, 32).start()
+
+    @pl.when(jnp.logical_not(is_main))
+    def _():
+        for k in steps:
+            y_copy(k, 8).start()
+
+    tiles_in[y] = tiles[y]
+
+    for copy in (loads[7], loads[9], loads[10]):
         copy.wait()
     for par in range(2):
         for q in range(2):
@@ -192,75 +277,31 @@
                             piece = jnp.zeros((16, CH), BF16)
                         wide[par * 2 + q, rows, :] = piece
 
-    row = lax.broadcasted_iota(jnp.int32, (256, TOK), 0)
-    token = lax.broadcasted_iota(jnp.int32, (256, TOK), 1)
-    t = row & 7
-    col = 2 * (((row >> 5) + 4) & 7) - 1 + ((row >> 3) & 3)
-    edge_row = jnp.where(t == 0, 5, jnp.where(t == 7, 0, -1))
-    main_row = jnp.where((t == 0) | (t == 7), -1, t - 1)
-    src_row = jnp.where(is_main, main_row, edge_row)
-    hit = (src_row >= 0) & (col >= 0) & (col < 16) & (token == src_row * 16 + col)
-    pick = jnp.where(hit, 1.0, 0.0).astype(BF16)
-
-    pl.semaphore_wait(near_sem, 6)
-    for device in beside_x:
-        pl.semaphore_signal(far_sem, inc=1, device_id=device, device_id_type=MESH)
-
     @pl.when(is_main)
     def _():
-        for k in (1, 3, 2):
-            slab_copy(k, 0).wait_recv()
+        for k in steps:
+            y_copy(k, 8 if k % 2 else 32).wait_recv()
 
     @pl.when(jnp.logical_not(is_main))
     def _():
-        for k in (1, 3, 2):
-            slab_copy(k, 64).wait_recv()
-
-    total = part[...] + part_in[0] + part_in[1] + part_in[2]
-    bias = bias_ref[...].reshape(1, 64)
-    patches = head_finish(total, jnp.concatenate([bias, bias], axis=1))
-    spread = jnp.dot(pick, patches, preferred_element_type=F32).astype(BF16)
-    tiles[...] = spread.reshape(CG, 32, 128)
-
-    c_copies = []
-    for k in (4, 3, 5, 2, 6, 1, 7):
-        to = lax.rem(y + k, CG)
-        c_copies.append(
-            pltpu.make_async_remote_copy(
-                src_ref=tiles.at[to],
-                dst_ref=tiles_in.at[y],
-                send_sem=c_send.at[k],
-                recv_sem=c_recv.at[k],
-                device_id=(group * CG + to, slab),
-                device_id_type=MESH,
-            )
-        )
-        c_copies[-1].start()
-    tiles_in[y] = tiles[y]
-
-    mid_swap = pltpu.make_async_remote_copy(
-        src_ref=mid_any,
-        dst_ref=midw.at[:, pl.ds(own_rows, SHARE), :],
-        send_sem=m_send,
-        recv_sem=m_recv,
-        device_id=(seq, half * 2 + 1 - core),
-        device_id_type=MESH,
-    )
-    mid_swap.start()
-
-    for copy in c_copies:
-        copy.wait_recv()
-    t32 = lax.broadcasted_iota(jnp.int32, (32, 128), 0) & 7
-    for f in range(2):
-        for b in range(2):
-            q = 2 * b + core
+        for k in steps:
+            y_copy(k, 32 if k % 2 else 8).wait_recv()
+
+    to_row = lax.broadcasted_iota(jnp.int32, (32, 48), 0)
+    from_row = lax.broadcasted_iota(jnp.int32, (32, 48), 1)
+    col2 = (to_row >> 3) * 2
+    t = to_row & 7
+    for b in range(2):
+        q = 2 * b + core
+        joined = (to_row == from_row) | ((t == 0) & (from_row == 32 + col2) & (q > 0))
+        joined = joined | ((t == 7) & (from_row == 41 + col2) & (q < 3))
+        join = jnp.where(joined, 1.0, 0.0).astype(BF16)
+        for f in range(2):
             main = tiles_in[4 * f + q].astype(F32)
-            above = tiles_in[4 * f + jnp.maximum(q - 1, 0)].astype(F32)
-            below = tiles_in[4 * f + jnp.minimum(q + 1, 3)].astype(F32)
-            value = main
-            value = value + jnp.where((t32 == 0) & (q > 0), above, 0.0)
-            value = value + jnp.where((t32 == 7) & (q < 3), below, 0.0)
-            block[f * 2 + b] = value.astype(BF16)
+            above = tiles_in[4 * f + jnp.maximum(q - 1, 0), 0:8].astype(F32)
+            below = tiles_in[4 * f + jnp.minimum(q + 1, 3), 0:8].astype(F32)
+            value = jnp.concatenate([main, above, below], axis=0).astype(BF16)
+            block[f * 2 + b] = jnp.dot(join, value, preferred_element_type=F32).astype(BF16)
 
     g_copies = []
     for d in (2, 1, 0):
@@ -281,14 +322,28 @@
     @pl.when(y < 4)
     def _():
         g_copies[2].start()
-        g_copies[2].wait()
 
     @pl.when(y >= 4)
     def _():
         grid[2] = block[...]
+
+    mid_swap = pltpu.make_async_remote_copy(
+        src_ref=mid_any,
+        dst_ref=midw.at[:, pl.ds(own_rows, SHARE), :],
+        send_sem=m_send,
+        recv_sem=m_recv,
+        device_id=(seq, half * 2 + 1 - core),
+        device_id_type=MESH,
+    )
+    mid_swap.start()
 
     g_copies[0].wait_recv()
     g_copies[1].wait_recv()
+
+    @pl.when(y < 4)
+    def _():
+        g_copies[2].wait()
+
 
     lane = lanes_of((2, 8, 128))
     low = lane < 64
@@ -374,31 +429,37 @@
     want = ((inner >> 2) & 1) * 64 + (inner & 3) * 16 + jnp.where(upper, 8, 0) + (inner >> 3)
     order = jnp.where(src == want, 1.0, 0.0).astype(BF16)
 
-    def mid_conv(block_of):
-        acc = jnp.zeros((128, CH), F32)
+    def mid_conv(block_of, lanes):
+        acc = jnp.zeros((128, lanes.stop - lanes.start), F32)
         for a in range(3):
             for b in range(3):
                 for c in range(3):
                     taken = acts[block_of, b : b + 2, c : c + 4, a].reshape(128, 256)
-                    acc = acc + jnp.dot(taken, midw[a * 9 + b * 3 + c], preferred_element_type=F32)
+                    weight = midw[a * 9 + b * 3 + c, :, lanes]
+                    acc = acc + jnp.dot(taken, weight, preferred_element_type=F32)
         return acc
 
-    other = mid_conv(1 - half).astype(BF16)
-    sums_out[...] = jnp.dot(order, other, preferred_element_type=F32).astype(BF16)
-    swap = pltpu.make_async_remote_copy(
-        src_ref=sums_out,
-        dst_ref=sums_in,
-        send_sem=r_send,
-        recv_sem=r_recv,
-        device_id=(seq, (1 - half) * 2 + core),
-        device_id_type=MESH,
-    )
-    swap.start()
-    mine = mid_conv(half) + resid[...].reshape(128, CH)
+    swaps = []
+    for n, lanes in enumerate((slice(0, CH),)):
+        other = mid_conv(1 - half, lanes).astype(BF16)
+        sums_out[:, lanes] = jnp.dot(order, other, preferred_element_type=F32).astype(BF16)
+        swaps.append(
+            pltpu.make_async_remote_copy(
+                src_ref=sums_out.at[:, lanes],
+                dst_ref=sums_in.at[:, lanes],
+                send_sem=r_send.at[n],
+                recv_sem=r_recv.at[n],
+                device_id=(seq, (1 - half) * 2 + core),
+                device_id_type=MESH,
+            )
+        )
+        swaps[-1].start()
+    mine = mid_conv(half, slice(0, CH)) + resid[...].reshape(128, CH)
     high = mine.astype(BF16)
     low_part = (mine - high.astype(F32)).astype(BF16)
     mine = jnp.dot(order, high, preferred_element_type=F32) + jnp.dot(order, low_part, preferred_element_type=F32)
-    swap.wait_recv()
+    for copy in swaps:
+        copy.wait_recv()
     out_ref[...] = (mine + sums_in[...].astype(F32)).astype(BF16)
 
     for k in (1, 2, 3):
@@ -412,20 +473,30 @@
         def _():
             slab_copy(k, 64).wait_send()
 
-    for copy in c_copies + g_copies[0:2]:
+    @pl.when(is_main)
+    def _():
+        for k in steps:
+            y_copy(k, 32).wait_send()
+
+    @pl.when(jnp.logical_not(is_main))
+    def _():
+        for k in steps:
+            y_copy(k, 8).wait_send()
+
+    for copy in sum_copies + g_copies[0:2]:
         copy.wait_send()
-    swap.wait_send()
+    for copy in swaps:
+        copy.wait_send()
 
 
 def shards(hidden, tangent, mod_shift, mod_scale, head_weight, head_bias, in_weight, in_bias, norm_gain, mid_weight):
     any_spec = pl.BlockSpec(memory_space=pl.ANY)
-    vmem = pl.BlockSpec(memory_space=pltpu.VMEM)
     dma = pltpu.SemaphoreType.DMA
     out = pl.pallas_call(
         kernel,
         out_shape=jax.ShapeDtypeStruct((TOK, CH), BF16),
         in_specs=[any_spec] * 10,
-        out_specs=vmem,
+        out_specs=pl.BlockSpec(memory_space=pltpu.VMEM),
         scratch_shapes=[
             pltpu.VMEM((TOK, DS), BF16),
             pltpu.VMEM((TOK, DS), BF16),
@@ -436,8 +507,10 @@
             pltpu.VMEM((64,), F32),
             pltpu.VMEM((CH,), F32),
             pltpu.VMEM((CH,), F32),
-            pltpu.VMEM((TOK + 16, 128), F32),
-            pltpu.VMEM((3, TOK + 16, 128), F32),
+            pltpu.VMEM((TOK, 128), BF16),
+            pltpu.VMEM((3, TOK, 128), BF16),
+            pltpu.VMEM((8, 128), F32),
+            pltpu.VMEM((3, 8, 128), F32),
             pltpu.VMEM((CG, 32, 128), BF16),
             pltpu.VMEM((CG, 32, 128), BF16),
             pltpu.VMEM((4, 32, 128), BF16),
@@ -451,8 +524,10 @@
             pltpu.VMEM((TOK, CH), BF16),
             pltpu.SemaphoreType.REGULAR,
             pltpu.SemaphoreType.REGULAR,
-            dma((9,)),
+            dma((11,)),
             dma,
+            dma((3,)),
+            dma((3,)),
             dma((3,)),
             dma((3,)),
             dma((CG,)),
@@ -461,8 +536,8 @@
             dma((3,)),
             dma,
             dma,
-            dma,
-            dma,
+            dma((1,)),
+            dma((1,)),
         ],
         compiler_params=pltpu.CompilerParams(collective_id=0, has_side_effects=True),
         name="decode",

time: 37.6 us -> 37.4 us (level)
  the two profiles are of different devices: /device:TPU:8 before, /device:TPU:64 now
where the time goes in v3:
time: 37.4 us; the launch traced here: 37.2 us
  Pallas kernels  35.7 us (95%)
  local copies, waits for them, and re-layouts  1.54 us (4%)
    pallas_call x1, Pallas kernels, shards(): pl.pallas_call(kernel, out_shape=jax.ShapeDtypeStruct((TOK, CH), BF16), i...  35.7 us
    reshape x1, local copies, waits for them, and re-layouts, shards(): return out.reshape(1, 2, 12, 4, CH)  1.54 us

profile of v3, /device:TPU:64, one launch (start us, length us, event | category | flops | bytes accessed | tf_op | source)
XLA Modules:
  0.0 37.2 jit_solution(3309046578198911884)
XLA Ops:
  0.0 35.7 %decode.1 = bf16[96,384]{1,0:T(8,128)(2,1)} custom-call(bf16[96,1280]{1,0:T(8,128)(2,1)} %x_any.1, bf16[96,1280]{1,0:T(8,128)(2,1)} %dx_any.1, f32[1280]{0:T(1024)} %shift_any.1, f32[1280]{0:T(1024)} %scale_any.1, bf16[64,1280]{1,0:T(8,128)(2,1)} %hw_any.1, f32[64]{0:T(128)} %bias_any.1, bf16[27,16,384]{2,1,0:T(8,128)(2,1)} %bitcast.3, f32[384]{0:T(512)} %inb_any.1, ...), custom_call_target="tpu_custom_call" | custom-call | tf_op jit(solution)/shard_map/decode/pallas_call | solution.py:495
  35.7 1.5 %reshape.11 = bf16[1,2,12,4,384]{4,3,2,1,0:T(4,128)(2,1)} reshape(bf16[96,384]{1,0:T(8,128)(2,1)} %decode.1) | data formatting | bytes 147456 | tf_op jit(solution)/shard_map/reshape | solution.py:556

commit v4 on v3

--- a/solution.py
+++ b/solution.py
@@ -316,8 +316,12 @@
             )
         )
     pl.semaphore_wait(far_sem, 2)
-    g_copies[0].start()
-    g_copies[1].start()
+    for copy, d in ((g_copies[0], 2), (g_copies[1], 1)):
+
+        @pl.when(group + d < GROUPS)
+        def _():
+            copy.start()
+
 
     @pl.when(y < 4)
     def _():
@@ -337,8 +341,16 @@
     )
     mid_swap.start()
 
-    g_copies[0].wait_recv()
-    g_copies[1].wait_recv()
+    for copy, d in ((g_copies[0], 2), (g_copies[1], 1)):
+
+        @pl.when(tile_group >= d)
+        def _():
+            copy.wait_recv()
+
+        @pl.when(tile_group < d)
+        def _():
+            grid[2 - d] = jnp.zeros((4, 32, 128), BF16)
+
 
     @pl.when(y < 4)
     def _():
@@ -348,11 +360,10 @@
     lane = lanes_of((2, 8, 128))
     low = lane < 64
     for slot in range(3):
-        keep = jnp.where(tile_group >= 2 - slot, 1.0, 0.0)
         for f in range(2):
             cols = []
             turned = []
-            cell = grid[slot, 2 * f : 2 * f + 2].astype(F32).reshape(2, 4, 8, 128) * keep
+            cell = grid[slot, 2 * f : 2 * f + 2].astype(F32).reshape(2, 4, 8, 128)
             for w in range(4):
                 value = cell[:, w]
                 cols.append(value)
@@ -483,8 +494,14 @@
         for k in steps:
             y_copy(k, 8).wait_send()
 
-    for copy in sum_copies + g_copies[0:2]:
+    for copy in sum_copies:
         copy.wait_send()
+    for copy, d in ((g_copies[0], 2), (g_copies[1], 1)):
+
+        @pl.when(group + d < GROUPS)
+        def _():
+            copy.wait_send()
+
     for copy in swaps:
         copy.wait_send()
 

time: 37.4 us -> 36 us (0.963)
  Pallas kernels: 35.7 us -> 34.3 us
    pallas_call x1, Pallas kernels: 35.7 us -> 34.3 us  [shards(): pl.pallas_call(kernel, out_shape=jax.ShapeDtypeStruct((TOK, CH), BF16), i...]
where the time goes in v4:
time: 36 us; the launch traced here: 35.8 us
  Pallas kernels  34.3 us (95%)
  local copies, waits for them, and re-layouts  1.54 us (4%)
    pallas_call x1, Pallas kernels, shards(): pl.pallas_call(kernel, out_shape=jax.ShapeDtypeStruct((TOK, CH), BF16), i...  34.3 us
    reshape x1, local copies, waits for them, and re-layouts, shards(): return out.reshape(1, 2, 12, 4, CH)  1.54 us

profile of v4, /device:TPU:64, one launch (start us, length us, event | category | flops | bytes accessed | tf_op | source)
XLA Modules:
  0.0 35.8 jit_solution(10028938301437211505)
XLA Ops:
  0.0 34.3 %decode.1 = bf16[96,384]{1,0:T(8,128)(2,1)} custom-call(bf16[96,1280]{1,0:T(8,128)(2,1)} %x_any.1, bf16[96,1280]{1,0:T(8,128)(2,1)} %dx_any.1, f32[1280]{0:T(1024)} %shift_any.1, f32[1280]{0:T(1024)} %scale_any.1, bf16[64,1280]{1,0:T(8,128)(2,1)} %hw_any.1, f32[64]{0:T(128)} %bias_any.1, bf16[27,16,384]{2,1,0:T(8,128)(2,1)} %bitcast.3, f32[384]{0:T(512)} %inb_any.1, ...), custom_call_target="tpu_custom_call" | custom-call | tf_op jit(solution)/shard_map/decode/pallas_call | solution.py:512
  34.3 1.5 %reshape.11 = bf16[1,2,12,4,384]{4,3,2,1,0:T(4,128)(2,1)} reshape(bf16[96,384]{1,0:T(8,128)(2,1)} %decode.1) | data formatting | bytes 147456 | tf_op jit(solution)/shard_map/reshape | solution.py:573

commit v5 on v4

--- a/solution.py
+++ b/solution.py
@@ -261,6 +261,70 @@
 
     tiles_in[y] = tiles[y]
 
+    @pl.when(is_main)
+    def _():
+        for k in steps:
+            y_copy(k, 8 if k % 2 else 32).wait_recv()
+
+    @pl.when(jnp.logical_not(is_main))
+    def _():
+        for k in steps:
+            y_copy(k, 32 if k % 2 else 8).wait_recv()
+
+    to_row = lax.broadcasted_iota(jnp.int32, (32, 48), 0)
+    from_row = lax.broadcasted_iota(jnp.int32, (32, 48), 1)
+    col2 = (to_row >> 3) * 2
+    t = to_row & 7
+    for b in range(2):
+        q = 2 * b + core
+        joined = (to_row == from_row) | ((t == 0) & (from_row == 32 + col2) & (q > 0))
+        joined = joined | ((t == 7) & (from_row == 41 + col2) & (q < 3))
+        join = jnp.where(joined, 1.0, 0.0).astype(BF16)
+        for f in range(2):
+            main = tiles_in[4 * f + q].astype(F32)
+            above = tiles_in[4 * f + jnp.maximum(q - 1, 0), 0:8].astype(F32)
+            below = tiles_in[4 * f + jnp.minimum(q + 1, 3), 0:8].astype(F32)
+            value = jnp.concatenate([main, above, below], axis=0).astype(BF16)
+            block[f * 2 + b] = jnp.dot(join, value, preferred_element_type=F32).astype(BF16)
+
+    g_copies = []
+    for d in (2, 1, 0):
+        g_copies.append(
+            pltpu.make_async_remote_copy(
+                src_ref=block,
+                dst_ref=grid.at[2 - d],
+                send_sem=g_send.at[d],
+                recv_sem=g_recv.at[d],
+                device_id=(lax.rem(group + d + late, GROUPS) * CG + y, slab),
+                device_id_type=MESH,
+            )
+        )
+    pl.semaphore_wait(far_sem, 2)
+    for copy, d in ((g_copies[0], 2), (g_copies[1], 1)):
+
+        @pl.when(group + d < GROUPS)
+        def _():
+            copy.start()
+
+
+    @pl.when(y < 4)
+    def _():
+        g_copies[2].start()
+
+    @pl.when(y >= 4)
+    def _():
+        grid[2] = block[...]
+
+    mid_swap = pltpu.make_async_remote_copy(
+        src_ref=mid_any,
+        dst_ref=midw.at[:, pl.ds(own_rows, SHARE), :],
+        send_sem=m_send,
+        recv_sem=m_recv,
+        device_id=(seq, half * 2 + 1 - core),
+        device_id_type=MESH,
+    )
+    mid_swap.start()
+
     for copy in (loads[7], loads[9], loads[10]):
         copy.wait()
     for par in range(2):
@@ -276,70 +340,6 @@
                         else:
                             piece = jnp.zeros((16, CH), BF16)
                         wide[par * 2 + q, rows, :] = piece
-
-    @pl.when(is_main)
-    def _():
-        for k in steps:
-            y_copy(k, 8 if k % 2 else 32).wait_recv()
-
-    @pl.when(jnp.logical_not(is_main))
-    def _():
-        for k in steps:
-            y_copy(k, 32 if k % 2 else 8).wait_recv()
-
-    to_row = lax.broadcasted_iota(jnp.int32, (32, 48), 0)
-    from_row = lax.broadcasted_iota(jnp.int32, (32, 48), 1)
-    col2 = (to_row >> 3) * 2
-    t = to_row & 7
-    for b in range(2):
-        q = 2 * b + core
-        joined = (to_row == from_row) | ((t == 0) & (from_row == 32 + col2) & (q > 0))
-        joined = joined | ((t == 7) & (from_row == 41 + col2) & (q < 3))
-        join = jnp.where(joined, 1.0, 0.0).astype(BF16)
-        for f in range(2):
-            main = tiles_in[4 * f + q].astype(F32)
-            above = tiles_in[4 * f + jnp.maximum(q - 1, 0), 0:8].astype(F32)
-            below = tiles_in[4 * f + jnp.minimum(q + 1, 3), 0:8].astype(F32)
-            value = jnp.concatenate([main, above, below], axis=0).astype(BF16)
-            block[f * 2 + b] = jnp.dot(join, value, preferred_element_type=F32).astype(BF16)
-
-    g_copies = []
-    for d in (2, 1, 0):
-        g_copies.append(
-            pltpu.make_async_remote_copy(
-                src_ref=block,
-                dst_ref=grid.at[2 - d],
-                send_sem=g_send.at[d],
-                recv_sem=g_recv.at[d],
-                device_id=(lax.rem(group + d + late, GROUPS) * CG + y, slab),
-                device_id_type=MESH,
-            )
-        )
-    pl.semaphore_wait(far_sem, 2)
-    for copy, d in ((g_copies[0], 2), (g_copies[1], 1)):
-
-        @pl.when(group + d < GROUPS)
-        def _():
-            copy.start()
-
-
-    @pl.when(y < 4)
-    def _():
-        g_copies[2].start()
-
-    @pl.when(y >= 4)
-    def _():
-        grid[2] = block[...]
-
-    mid_swap = pltpu.make_async_remote_copy(
-        src_ref=mid_any,
-        dst_ref=midw.at[:, pl.ds(own_rows, SHARE), :],
-        send_sem=m_send,
-        recv_sem=m_recv,
-        device_id=(seq, half * 2 + 1 - core),
-        device_id_type=MESH,
-    )
-    mid_swap.start()
 
     for copy, d in ((g_copies[0], 2), (g_copies[1], 1)):
 

time: 36 us -> 36 us (level)
  no operation moved by 1% of the time
where the time goes in v5:
time: 36 us; the launch traced here: 35.8 us
  Pallas kernels  34.3 us (95%)
  local copies, waits for them, and re-layouts  1.54 us (4%)
    pallas_call x1, Pallas kernels, shards(): pl.pallas_call(kernel, out_shape=jax.ShapeDtypeStruct((TOK, CH), BF16), i...  34.3 us
    reshape x1, local copies, waits for them, and re-layouts, shards(): return out.reshape(1, 2, 12, 4, CH)  1.54 us

profile of v5, /device:TPU:64, one launch (start us, length us, event | category | flops | bytes accessed | tf_op | source)
XLA Modules:
  0.0 35.8 jit_solution(14564731328793753572)
XLA Ops:
  0.0 34.3 %decode.1 = bf16[96,384]{1,0:T(8,128)(2,1)} custom-call(bf16[96,1280]{1,0:T(8,128)(2,1)} %x_any.1, bf16[96,1280]{1,0:T(8,128)(2,1)} %dx_any.1, f32[1280]{0:T(1024)} %shift_any.1, f32[1280]{0:T(1024)} %scale_any.1, bf16[64,1280]{1,0:T(8,128)(2,1)} %hw_any.1, f32[64]{0:T(128)} %bias_any.1, bf16[27,16,384]{2,1,0:T(8,128)(2,1)} %bitcast.3, f32[384]{0:T(512)} %inb_any.1, ...), custom_call_target="tpu_custom_call" | custom-call | tf_op jit(solution)/shard_map/decode/pallas_call | solution.py:512
  34.3 1.5 %reshape.11 = bf16[1,2,12,4,384]{4,3,2,1,0:T(4,128)(2,1)} reshape(bf16[96,384]{1,0:T(8,128)(2,1)} %decode.1) | data formatting | bytes 147456 | tf_op jit(solution)/shard_map/reshape | solution.py:573

commit v6 on v5

--- a/solution.py
+++ b/solution.py
@@ -160,9 +160,6 @@
 
     for copy in loads[0:7]:
         copy.wait()
-    for copy in loads[7:]:
-        copy.start()
-    mid_copy.start()
     own = head_partials(xv, dxv, hwv, scale_ref, shift_ref, part, sums)
 
     quarter = lax.rem(y, 4)
@@ -201,6 +198,9 @@
         @pl.when(jnp.logical_not(to_main))
         def _():
             slab_copy(k, 64).start()
+
+    for copy in loads[7:]:
+        copy.start()
 
     row = lax.broadcasted_iota(jnp.int32, (256, TOK), 0)
     token = lax.broadcasted_iota(jnp.int32, (256, TOK), 1)
@@ -323,6 +323,7 @@
         device_id=(seq, half * 2 + 1 - core),
         device_id_type=MESH,
     )
+    mid_copy.start()
     mid_swap.start()
 
     for copy in (loads[7], loads[9], loads[10]):

time: 36 us -> 36 us (level)
  no operation moved by 1% of the time
where the time goes in v6:
time: 36 us; the launch traced here: 35.8 us
  Pallas kernels  34.3 us (95%)
  local copies, waits for them, and re-layouts  1.54 us (4%)
    pallas_call x1, Pallas kernels, shards(): pl.pallas_call(kernel, out_shape=jax.ShapeDtypeStruct((TOK, CH), BF16), i...  34.3 us
    reshape x1, local copies, waits for them, and re-layouts, shards(): return out.reshape(1, 2, 12, 4, CH)  1.54 us

profile of v6, /device:TPU:64, one launch (start us, length us, event | category | flops | bytes accessed | tf_op | source)
XLA Modules:
  0.0 35.8 jit_solution(6104049510382236382)
XLA Ops:
  0.0 34.3 %decode.1 = bf16[96,384]{1,0:T(8,128)(2,1)} custom-call(bf16[96,1280]{1,0:T(8,128)(2,1)} %x_any.1, bf16[96,1280]{1,0:T(8,128)(2,1)} %dx_any.1, f32[1280]{0:T(1024)} %shift_any.1, f32[1280]{0:T(1024)} %scale_any.1, bf16[64,1280]{1,0:T(8,128)(2,1)} %hw_any.1, f32[64]{0:T(128)} %bias_any.1, bf16[27,16,384]{2,1,0:T(8,128)(2,1)} %bitcast.3, f32[384]{0:T(512)} %inb_any.1, ...), custom_call_target="tpu_custom_call" | custom-call | tf_op jit(solution)/shard_map/decode/pallas_call | solution.py:513
  34.3 1.5 %reshape.11 = bf16[1,2,12,4,384]{4,3,2,1,0:T(4,128)(2,1)} reshape(bf16[96,384]{1,0:T(8,128)(2,1)} %decode.1) | data formatting | bytes 147456 | tf_op jit(solution)/shard_map/reshape | solution.py:574
